TPU v7x, 128 devices: a whole 4x4x4 slice. The times are simulated.
128 devices in a mesh: store: 16 (over x, y), ctx: 8 (over z, core).
Axes of the slice: x: 4, y: 4, z: 4, core: 2. Of those that a mesh axis runs over, the one named last changes fastest.
Arguments:
- tokens: bfloat16 [2048, 8192], P('store'), may hold values from -6 to 6
- joined_weight: bfloat16 [8192, 8, 1280], P(None, 'ctx'), may hold values from -0.0625 to 0.0625
- down_weight: bfloat16 [128, 8192, 64], P('store', 'ctx'), may hold values from -0.0625 to 0.0625
- up_weight: bfloat16 [128, 64, 8, 1280], P('store', None, 'ctx'), may hold values from -0.75 to 0.75
- adapter_per_request: int32 [2048], replicated, may hold values from 0 to 127, as said below
- adapter_store_slot: int32 [128], replicated, may hold values from 0 to 127, as said below
- prefix_block_list: int32 [2048, 8], P('store'), may hold values from 0 to 255, as said below
- prefix_length: int32 [2048], P('store'), may hold values from 1 to 128, as said below
- key_value_pool: bfloat16 [4096, 8, 256], P(('store', 'ctx')), may hold values from -400 to 400
Outputs:
- attn: bfloat16 [2048, 8, 1024], P('store', 'ctx')
Inputs may be any that keep to these rules, and one draw needn't show every extreme that they name: `adapter_store_slot`: A permutation; slot s belongs to owner s // 8, which holds slots in store order. `adapter_per_request`: among the 128 requests of one store shard, at most 16 use adapters of one owner; on every shard one owner, the same for all shards, receives exactly 16. `prefix_block_list`: the 8 blocks of a request are distinct and lie in its store shard's range of 16 blocks, rows i * 128 to (i+1) * 128 - 1 using blocks i * 16 to (i+1) * 16 - 1. `prefix_length`: every store shard has a request of length 128.
All inputs are finite; a program needn't handle non-finite values.
Results may differ from a plain program's by a relative error of at most 0.02.
The roundings to bfloat16 on the way count: a program that leaves them out, or rounds other values in their place, can miss the bound.
Values may be sent and summed in bfloat16 or wider, within the bound.
No kernel may reach another device: no remote copies, remote signals or barrier semaphores. Data moves between devices by JAX's collectives and lax.ppermute only.
A program may use at most 128 MiB of HBM per device.

v0:
```python
import jax
import jax.numpy as jnp
from jax import lax
from jax.sharding import PartitionSpec as P

QUERY_PER_KEY = 8
HEAD_SIZE = 128
CAP = 16
BLK = 16


ROPE_THETA = 500000.0
ADAPTER_SCALE = 2.0


def rotary_apply(vec, token_position):
    half = vec.shape[-1] // 2
    freq = jnp.power(ROPE_THETA, -(jnp.arange(half, dtype=jnp.float32) * 2.0 / vec.shape[-1]))
    angle = token_position[..., None] * freq
    cosine = jnp.cos(angle)
    sine = jnp.sin(angle)
    initial_part = vec[..., :half]
    second = vec[..., half:]
    return jnp.concatenate(
        [initial_part * cosine - second * sine, initial_part * sine + second * cosine], axis=-1
    )


def prefix_mask(local_ids, lens, group_blocks, blk):
    listed = local_ids.shape[1]
    equal = local_ids[:, :, None] == jnp.arange(group_blocks, dtype=jnp.int32)[None, None, :]
    start = jnp.sum(
        jnp.where(equal, (jnp.arange(listed, dtype=jnp.int32) * blk)[None, :, None], 0), axis=1
    )
    present = jnp.any(equal, axis=1)
    offset = jnp.arange(blk, dtype=jnp.int32)
    live = present[:, :, None] & (start[:, :, None] + offset[None, None, :] < lens[:, None, None])
    return live.reshape(local_ids.shape[0], group_blocks * blk)


def attend(query_rows, key_new, value_new, keys, value_rows, live):
    scale = 1.0 / HEAD_SIZE**0.5
    pool_scores = (
        jnp.einsum("rhgd,thd->rhgt", query_rows, keys, preferred_element_type=jnp.float32) * scale
    )
    own = (
        jnp.einsum("rhgd,rhd->rhg", query_rows, key_new, preferred_element_type=jnp.float32) * scale
    )
    mask = live[:, None, None, :]
    pool_scores = jnp.where(mask, pool_scores, -jnp.inf)
    top = jnp.maximum(jnp.max(pool_scores, axis=-1), own)
    prob = jnp.where(mask, jnp.exp(pool_scores - top[..., None]), 0.0)
    prob_own = jnp.exp(own - top)
    total = jnp.sum(prob, axis=-1) + prob_own
    prob_low = prob.astype(jnp.bfloat16)
    own_low = prob_own.astype(jnp.bfloat16)
    mixed = jnp.einsum("rhgt,thd->rhgd", prob_low, value_rows, preferred_element_type=jnp.float32)
    mixed = (
        mixed
        + own_low.astype(jnp.float32)[..., None] * value_new.astype(jnp.float32)[:, :, None, :]
    )
    mixed = mixed / total[..., None]
    return mixed.astype(jnp.bfloat16).reshape(query_rows.shape[0], query_rows.shape[1], -1)


def routing(adapter_per_request, adapter_store_slot, shards, request_shard, shard_adapters):
    adapters = adapter_store_slot.shape[0]
    match = adapter_per_request[:, None] == jnp.arange(adapters, dtype=jnp.int32)[None, :]
    store_slot = jnp.sum(jnp.where(match, adapter_store_slot[None, :], 0), axis=1).reshape(
        shards, request_shard
    )
    owner = store_slot // shard_adapters
    owner_hot = (owner[:, :, None] == jnp.arange(shards, dtype=jnp.int32)[None, None, :]).astype(
        jnp.int32
    )
    counted = jnp.cumsum(owner_hot, axis=1) - 1
    rank = jnp.sum(owner_hot * counted, axis=2)
    return (store_slot, owner, rank)


def body(
    tokens,
    joined_weight,
    down_weight,
    up_weight,
    adapter_per_request,
    adapter_store_slot,
    prefix_block_list,
    prefix_length,
    key_value_pool,
):
    n_store = lax.axis_size("store")
    n_ctx = lax.axis_size("ctx")
    shard = lax.axis_index("store")
    member = lax.axis_index("ctx")
    request_shard = tokens.shape[0]
    d_model = tokens.shape[1]
    shard_adapters = down_weight.shape[0]
    width_slice = down_weight.shape[1]
    head_slice = joined_weight.shape[1]
    column_list = joined_weight.shape[2]
    whole_group = lax.all_gather(key_value_pool, "ctx", axis=0, tiled=True)
    group = lax.dynamic_slice_in_dim(whole_group, member * head_slice, head_slice, 1)
    store_slot, owner, rank = routing(
        adapter_per_request, adapter_store_slot, n_store, request_shard, shard_adapters
    )
    owner_mine = lax.dynamic_index_in_dim(owner, shard, 0, keepdims=False)
    rank_mine = lax.dynamic_index_in_dim(rank, shard, 0, keepdims=False)
    dest = owner_mine * CAP + rank_mine
    x_local = lax.dynamic_slice_in_dim(tokens, member * width_slice, width_slice, 1)
    outgoing = jnp.zeros((n_store * CAP, width_slice), jnp.bfloat16).at[dest].set(x_local)
    received_parts = lax.all_to_all(
        outgoing.reshape(n_store, CAP, width_slice),
        "store",
        split_axis=0,
        concat_axis=0,
        tiled=True,
    )
    local_slot = store_slot % shard_adapters
    selected = (owner == shard)[:, :, None] & (
        rank[:, :, None] == jnp.arange(CAP, dtype=jnp.int32)[None, None, :]
    )
    adapter_hot = selected[:, :, :, None] & (
        local_slot[:, :, None, None]
        == jnp.arange(shard_adapters, dtype=jnp.int32)[None, None, None, :]
    )
    adapter_hot = jnp.any(adapter_hot, axis=1)
    value_partial = jnp.einsum(
        "hbm,gmq->hbgq", received_parts, down_weight, preferred_element_type=jnp.float32
    )
    shrunk_part = jnp.sum(jnp.where(adapter_hot[..., None], value_partial, 0.0), axis=2)
    shrunk = lax.psum(shrunk_part, "ctx").astype(jnp.bfloat16)
    spread_rows = jnp.where(
        adapter_hot[..., None], shrunk[:, :, None, :], jnp.zeros((), jnp.bfloat16)
    )
    adapter_update = jnp.einsum(
        "oxbl,blpj->oxpj", spread_rows, up_weight, preferred_element_type=jnp.float32
    ).astype(jnp.bfloat16)
    returned = lax.all_to_all(adapter_update, "store", split_axis=0, concat_axis=0, tiled=True)
    update_mine = returned.reshape(n_store * CAP, head_slice, column_list)[dest]
    plain_projection = jnp.dot(
        tokens,
        joined_weight.reshape(d_model, head_slice * column_list),
        preferred_element_type=jnp.float32,
    )
    joined_projection = plain_projection.reshape(
        request_shard, head_slice, column_list
    ) + ADAPTER_SCALE * update_mine.astype(jnp.float32)
    token_position = prefix_length.astype(jnp.float32)
    query_rows = rotary_apply(
        joined_projection[:, :, : QUERY_PER_KEY * HEAD_SIZE].reshape(
            request_shard, head_slice, QUERY_PER_KEY, HEAD_SIZE
        ),
        token_position[:, None, None],
    ).astype(jnp.bfloat16)
    key_new = rotary_apply(
        joined_projection[:, :, QUERY_PER_KEY * HEAD_SIZE : (QUERY_PER_KEY + 1) * HEAD_SIZE],
        token_position[:, None],
    ).astype(jnp.bfloat16)
    value_new = joined_projection[:, :, (QUERY_PER_KEY + 1) * HEAD_SIZE :].astype(jnp.bfloat16)
    group_blocks = key_value_pool.shape[0] * n_ctx // BLK
    live = prefix_mask(prefix_block_list - shard * group_blocks, prefix_length, group_blocks, BLK)
    return attend(
        query_rows, key_new, value_new, group[:, :, :HEAD_SIZE], group[:, :, HEAD_SIZE:], live
    )


def solution(mesh):
    in_specs = (
        P("store", None),
        P(None, "ctx", None),
        P("store", "ctx", None),
        P("store", None, "ctx", None),
        P(),
        P(),
        P("store", None),
        P("store"),
        P(("store", "ctx"), None, None),
    )
    out_specs = P("store", "ctx", None)
    return jax.shard_map(body, mesh=mesh, in_specs=in_specs, out_specs=out_specs, check_vma=False)
```

profile of v0, /device:TPU:0, one launch (start us, length us, event | category | flops | bytes accessed | tf_op | source)
XLA Modules:
  0.0 103.6 jit_solution(7977212411898777867)
XLA Ops:
  6.5 1.7 %copy.72 = bf16[32,8,256]{2,0,1:T(8,128)(2,1)} copy(bf16[32,8,256]{2,1,0:T(8,128)(2,1)} %param.17) | data formatting | bytes 262144 | tf_op args[8]
  8.3 1.3 %select_reduce_fusion.1 = s32[2048]{0:T(1024)S(1)} fusion(s32[128]{0:T(128)} %param.14, s32[2048]{0:T(1024)} %param.13), kind=kLoop, calls=%fused_computation.25 | loop fusion | flops 784384 | bytes 16896 | tf_op jit(solution)/shard_map/reduce_sum | solution.py:69
  9.8 2.8 %select_reduce_fusion = s32[16,128]{0,1:T(8,128)S(1)} fusion(s32[16,128]{0,1:T(8,128)S(1)} %copy.73), kind=kOutput, calls=%fused_computation.21 | output fusion | flops 4356096 | bytes 16384 | tf_op jit(solution)/shard_map/jit(cumsum)/reduce_window_sum | solution.py:76
  12.7 2.0 %scatter_custom_fusion = bf16[256,1024]{1,0:T(8,128)(2,1)} fusion(s32[128]{0:T(128)S(1)} %fusion.66, bf16[128,8192]{1,0:T(8,128)(2,1)S(1)} %copy-done, s32[]{:T(128)} %constant.35.clone.1, s32[]{:T(128)S(6)} %select_n.75, bf16[]{:T(256)} %constant.73.clone.1), kind=kCustom, calls=%fused_computation.46 | custom fusion | bytes 786442 | tf_op jit(solution)/shard_map/scatter | solution.py:111
  14.6 7.1 %all-to-all-start = ((bf16[16,16,1024]{2,1,0:T(8,128)(2,1)}), bf16[16,16,1024]{2,1,0:T(8,128)(2,1)S(1)}, u32[]{:S(2)}, u32[]{:S(2)}) async-start(bf16[16,16,1024]{2,1,0:T(8,128)(2,1)} %bitcast.10), calls=%async_computation | async-start | bytes 1048576 | tf_op jit(solution)/shard_map/all_to_all | solution.py:112
  21.9 4.4 %and_reduce_fusion = pred[16,16,8]{2,1,0:T(8,128)(4,1)S(1)} fusion(pred[16,128,8]{1,2,0:T(8,128)(4,1)S(1)} %iota_compare_fusion.4, pred[16,128,16]{1,2,0:T(8,128)(4,1)S(1)} %fusion.41), kind=kLoop, calls=%fused_computation.27 | loop fusion | flops 522240 | bytes 51200 | tf_op jit(solution)/shard_map/reduce_or | solution.py:127
  26.5 6.8 %all-to-all-done = bf16[16,16,1024]{2,1,0:T(8,128)(2,1)S(1)} async-done(((bf16[16,16,1024]{2,1,0:T(8,128)(2,1)}), bf16[16,16,1024]{2,1,0:T(8,128)(2,1)S(1)}, u32[]{:S(2)}, u32[]{:S(2)}) %all-to-all-start) | async-done | bytes 524320 | tf_op jit(solution)/shard_map/all_to_all | solution.py:112
  33.3 2.0 %fusion.12 = f32[16,16,64]{2,1,0:T(8,128)S(1)} fusion(bf16[8,1024,64]{1,2,0:T(8,128)(2,1)} %param.11, bf16[16,16,1024]{2,1,0:T(8,128)(2,1)S(1)} %all-to-all-done, pred[16,16,8]{1,2,0:T(8,128)(4,1)S(1)} %copy.75), kind=kOutput, calls=%fused_computation.13 | convolution fusion | flops 268681216 | bytes 1640448 | tf_op jit(solution)/shard_map/hbm,gmq->hbgq/dot_general | solution.py:128
  35.3 26.7 %psum.7 = bf16[16,16,64]{2,1,0:T(8,128)(2,1)S(1)} all-reduce(f32[16,16,64]{2,1,0:T(8,128)S(1)} %fusion.12), channel_id=1, replica_groups=mesh['store'=16,'ctx'=8] {'ctx'}, use_global_device_ids=true, to_apply=%region_8.9 | all-reduce | flops 16384 | bytes 98304 | tf_op jit(solution)/shard_map/psum | solution.py:132
  62.0 3.0 %fusion.6 = bf16[16,16,1,1280]{3,1,2,0:T(8,128)(2,1)} fusion(bf16[8,64,1,1280]{3,1,2,0:T(8,128)(2,1)} %param.12, pred[16,16,8]{1,2,0:T(8,128)(4,1)S(1)} %copy.75, bf16[16,16,64]{2,1,0:T(8,128)(2,1)S(1)} %psum.7), kind=kOutput, calls=%fused_computation.7 | convolution fusion | flops 336003072 | bytes 2000896 | tf_op jit(solution)/shard_map/oxbl,blpj->oxpj/dot_general | solution.py:136
  65.0 3.8 %all-to-all-start.1 = ((bf16[16,16,1,1280]{3,1,2,0:T(8,128)(2,1)}), bf16[16,16,1,1280]{3,1,2,0:T(8,128)(2,1)S(1)}, u32[]{:S(2)}, u32[]{:S(2)}) async-start(bf16[16,16,1,1280]{3,1,2,0:T(8,128)(2,1)} %fusion.6), calls=%async_computation.1 | async-start | bytes 1310720 | tf_op jit(solution)/shard_map/all_to_all | solution.py:139
  69.1 0.3 multiply_cosine_fusion.1
  69.4 10.1 %all-to-all-done.1 = bf16[16,16,1,1280]{3,1,2,0:T(8,128)(2,1)S(1)} async-done(((bf16[16,16,1,1280]{3,1,2,0:T(8,128)(2,1)}), bf16[16,16,1,1280]{3,1,2,0:T(8,128)(2,1)S(1)}, u32[]{:S(2)}, u32[]{:S(2)}) %all-to-all-start.1) | async-done | bytes 655392 | tf_op jit(solution)/shard_map/all_to_all | solution.py:139
  79.5 1.6 %gather_fusion = bf16[128,1280]{1,0:T(8,128)(2,1)} fusion(bf16[256,1280]{1,0:T(8,128)(2,1)S(1)} %bitcast.144, s32[1024]{0:T(1024)S(1)} %pad_clamp_fusion), kind=kCustom, calls=%fused_computation | custom fusion | bytes 655872 | tf_op jit(solution)/shard_map/gather | solution.py:140
  81.2 9.9 %fusion.7 = f32[128,1,1280]{2,0,1:T(8,128)S(1)} fusion(bf16[128,8192]{1,0:T(8,128)(2,1)S(1)} %copy-done, bf16[8192,1,1280]{2,0,1:T(8,128)(2,1)} %param.10, bf16[128,1280]{1,0:T(8,128)(2,1)} %gather_fusion), kind=kOutput, calls=%fused_computation.8 | convolution fusion | flops 2684846080 | bytes 24051712 | tf_op jit(solution)/shard_map/dot_general | solution.py:141
  91.2 0.7 copy.82
  91.9 0.3 fusion.56
  92.3 0.2 fusion.69
  92.5 0.2 fusion.31
  92.9 0.3 fusion.38
  93.3 1.2 %fusion.70 = (f32[128,8]{0,1:T(8,128)S(1)}, f32[128,1,8,256]{0,3,2,1:T(8,128)S(1)}) fusion(bf16[128,8,128]{2,0,1:T(8,128)(2,1)S(1)} %pad_maximum_fusion, bf16[256,8,256]{2,0,1:T(8,128)(2,1)} %all-gather.2.cloned.1.call-done, s32[]{:T(128)S(6)} %select_n.68, pred[128,256]{0,1:T(8,128)(4,1)S(1)} %fusion.42), kind=kOutput, calls=%fused_computation.112 | convolution fusion | flops 67894272 | bytes 1413124 | tf_op jit(solution)/shard_map/rhgd,thd->rhgt/dot_general | solution.py:44
  94.5 0.2 fusion.20
  94.7 1.2 %fusion.16 = bf16[128,1,8,128]{0,3,2,1:T(8,128)(2,1)S(1)} fusion(f32[128,1,8,256]{0,3,2,1:T(8,128)S(1)} %get-tuple-element.18, f32[128,8]{0,1:T(8,128)S(1)} %fusion.60, pred[128,256]{0,1:T(8,128)(4,1)S(1)} %fusion.42, f32[128,8]{0,1:T(8,128)S(1)} %get-tuple-element.12, f32[128,128]{0,1:T(8,128)S(1)} %copy-done.1, f32[128,8]{0,1:T(8,128)S(1)} %get-tuple-element.11, ...), kind=kOutput, calls=%fused_computation.18 | convolution fusion | flops 68419584 | bytes 1486856 | tf_op jit(solution)/shard_map/rhgt,thd->rhgd/dot_general | solution.py:57
  95.9 0.9 copy.83
  (37 shorter events, 1.2 us)
Async XLA Ops:
  6.5 6.1 %copy-start = (bf16[128,8192]{1,0:T(8,128)(2,1)S(1)}, bf16[128,8192]{1,0:T(8,128)(2,1)}, u32[]{:S(2)}) copy-start(bf16[128,8192]{1,0:T(8,128)(2,1)} %param.9) | copy-start | bytes 6291460
  6.5 19.9 %copy-start.2 = (s32[128,8]{0,1:T(8,128)S(1)}, s32[128,8]{0,1:T(8,128)}, u32[]{:S(2)}) copy-start(s32[128,8]{0,1:T(8,128)} %param.15) | copy-start | bytes 12292
  6.5 86.7 %all-gather.2.cloned.1.call-start = ((), (), s32[]{:S(2)}) async-start(), calls=%async_computation.2 | async-start | bytes 1179648 | tf_op jit(solution)/shard_map/all_gather | solution.py:102
  14.6 18.6 %all-to-all-start = ((bf16[16,16,1024]{2,1,0:T(8,128)(2,1)}), bf16[16,16,1024]{2,1,0:T(8,128)(2,1)S(1)}, u32[]{:S(2)}, u32[]{:S(2)}) async-start(bf16[16,16,1024]{2,1,0:T(8,128)(2,1)} %bitcast.10), calls=%async_computation | async-start | bytes 1048576 | tf_op jit(solution)/shard_map/all_to_all | solution.py:112
  62.0 6.8 %copy-start.3 = (s32[128]{0:T(128)S(1)}, s32[128]{0:T(128)}, u32[]{:S(2)}) copy-start(s32[128]{0:T(128)} %param.16) | copy-start | bytes 1540
  65.0 14.6 %all-to-all-start.1 = ((bf16[16,16,1,1280]{3,1,2,0:T(8,128)(2,1)}), bf16[16,16,1,1280]{3,1,2,0:T(8,128)(2,1)S(1)}, u32[]{:S(2)}, u32[]{:S(2)}) async-start(bf16[16,16,1,1280]{3,1,2,0:T(8,128)(2,1)} %fusion.6), calls=%async_computation.1 | async-start | bytes 1310720 | tf_op jit(solution)/shard_map/all_to_all | solution.py:139
  92.8 1.9 %copy-start.1 = (f32[128,128]{0,1:T(8,128)S(1)}, f32[128,128]{0,1:T(8,128)}, u32[]{:S(2)}) copy-start(f32[128,128]{0,1:T(8,128)} %copy.82) | copy-start | bytes 196612
Sparse Core Ops, SparseCore 0:
  9.1 26.0 all-gather.1
where the time goes:
time: 104 us
  blocking collectives  26.7 us (26%)
  matrix products  17.5 us (17%)
  waiting for transfers between devices  16.9 us (16%)
  between operations  13.7 us (13%)
  starting transfers between devices  10.9 us (10%)
  other arithmetic  10.2 us (10%)
  local copies, waits for them, and re-layouts  7.7 us (7%)
    psum x1, blocking collectives, body(): shrunk = lax.psum(shrunk_part, 'ctx').astype(jnp.bfloat16)  26.7 us
    all_to_all x1, waiting for transfers between devices, body(): lax.all_to_all(adapter_update, 'store', split_axis=0, concat_axis=0, tile...  10.1 us
    dot_general x1, matrix products, body(): jnp.dot(tokens, joined_weight.reshape(d_model, head_slice * column_list),...  9.86 us
    all_to_all x1, starting transfers between devices, body(): lax.all_to_all(outgoing.reshape(n_store, CAP, width_slice), 'store', spli...  7.12 us
    all_to_all x1, waiting for transfers between devices, body(): lax.all_to_all(outgoing.reshape(n_store, CAP, width_slice), 'store', spli...  6.79 us
    reduce_or x1, other arithmetic, body(): adapter_hot = jnp.any(adapter_hot, axis=1)  4.45 us
    all_to_all x1, starting transfers between devices, body(): lax.all_to_all(adapter_update, 'store', split_axis=0, concat_axis=0, tile...  3.81 us
    dot_general x1, matrix products, body(): jnp.einsum('oxbl,blpj->oxpj', spread_rows, up_weight, preferred_element_t...  2.99 us
  transfers between devices with their start and end apart: 3, of which 2 were waited for; matrix products, arithmetic and copies ran while one was open for 29% of the time, Pallas kernels for 0%

commit v1 on v0

v1 whole, which is shorter than its diff:
```python
import functools

import jax
import jax.numpy as jnp
import numpy as np
from jax import lax
from jax.experimental import pallas as pl
from jax.experimental.pallas import tpu as pltpu
from jax.sharding import PartitionSpec as P

QUERY_PER_KEY = 8
HEAD = 128
CAP = 16
BLK = 16
NZ = 4
ROPE_THETA = 500000.0
ADAPTER_SCALE = 2.0
BK = 512
STEPS_A = 8

F32 = jnp.float32
BF16 = jnp.bfloat16


def iota(shape, dim):
    return lax.broadcasted_iota(jnp.int32, shape, dim)


def before():
    return (iota((128, 128), 0) < iota((128, 128), 1)).astype(BF16)


def pack_kernel(adapter_ref, table_ref, tokens_ref, out_ref, dest_ref, x_ref, sem):
    shard = lax.axis_index("store")
    width = x_ref.shape[1]
    start = pl.multiple_of(lax.axis_index("ctx") * width, 128)
    copy = pltpu.make_async_copy(tokens_ref.at[:, pl.ds(start, width)], x_ref, sem)
    copy.start()
    shards = adapter_ref.shape[0]
    mine = jnp.broadcast_to(adapter_ref[pl.ds(shard, 1), :], (8, 128))
    table = jnp.broadcast_to(table_ref[...], (8, 128))
    slot = jnp.take_along_axis(table, mine, axis=1)[:1]
    owner = slot // 8
    hot = (owner == iota((shards, 128), 0)).astype(F32)
    counted = jnp.dot(hot.astype(BF16), before(), preferred_element_type=F32)
    rank = jnp.sum(hot * counted, axis=0, keepdims=True).astype(jnp.int32)
    dest = owner * CAP + rank
    dest_ref[...] = jnp.broadcast_to(dest, dest_ref.shape)
    place = (dest == iota((shards * CAP, 128), 0)).astype(F32).astype(BF16)
    copy.wait()
    out_ref[...] = jnp.dot(place, x_ref[...], preferred_element_type=F32).astype(BF16)


def first_kernel(adapter_ref, table_ref, pool_ref, x_ref, w_ref, acc_ref, local_ref, heads_ref):
    step = pl.program_id(0)

    @pl.when(step == 0)
    def _():
        shard = lax.axis_index("store")
        core = lax.axis_index("ctx") % 2
        shards = adapter_ref.shape[0]
        table = jnp.broadcast_to(table_ref[...], (shards, 128))
        slot = jnp.take_along_axis(table, adapter_ref[...], axis=1)
        sent = (slot // 8 == shard).astype(F32)
        rank = jnp.dot(sent.astype(BF16), before(), preferred_element_type=F32)
        rank = jnp.where(sent > 0, rank, -1.0)
        value = (slot % 8 + 1).astype(F32)
        position = iota((CAP, 128), 0).astype(F32)
        rows = [
            jnp.where(rank[h : h + 1] == position, value[h : h + 1], 0.0) for h in range(shards)
        ]
        column = jnp.sum(jnp.concatenate(rows, axis=0), axis=1, keepdims=True)
        n = shards * CAP
        square = jnp.where(iota((n, n), 0) == iota((n, n), 1), column, 0.0)
        local_ref[...] = jnp.broadcast_to(jnp.sum(square, axis=0, keepdims=True), local_ref.shape)
        row = iota((256, 256), 0)
        parity = jnp.where(row < 128, core, 1 - core)
        source = (row % 32) * 8 + ((row // 32) % NZ) * 2 + parity
        select = (source == iota((256, 256), 1)).astype(F32).astype(BF16)
        heads_ref[...] = jnp.dot(select, pool_ref[...], preferred_element_type=F32).astype(BF16)
        acc_ref[...] = jnp.zeros_like(acc_ref)

    acc_ref[...] += jnp.dot(x_ref[...], w_ref[...], preferred_element_type=F32)


def split_sum(x):
    high = x.astype(BF16)
    return high, (x - high.astype(F32)).astype(BF16)


def down_kernel(received_ref, down_ref, local_ref, heads_ref, part_ref, send_ref):
    every = lax.dot_general(
        down_ref[...], received_ref[...], (((1,), (1,)), ((), ())), preferred_element_type=F32
    )
    local = local_ref[:1]
    part = jnp.zeros(part_ref.shape, F32)
    for g in range(8):
        part = part + jnp.where(local == g + 1.0, every[g * 64 : (g + 1) * 64], 0.0)
    part_ref[...] = part
    high, low = split_sum(part)
    send_ref[:64] = high
    send_ref[64:128] = low
    send_ref[128:] = heads_ref[128:]


def middle_kernel(part_ref, heads_ref, other_ref, sum_ref, pool_ref, s1_ref, s2_ref, s3_ref):
    member = lax.axis_index("ctx")
    core = member % 2
    z = member // 2
    total = part_ref[...] + (other_ref[:64].astype(F32) + other_ref[64:128].astype(F32))
    sum_ref[...] = total
    high, low = split_sum(total)
    mine = pl.multiple_of(core * 32, 32)
    theirs = pl.multiple_of((1 - core) * 32, 32)
    for j, ref, base in ((0, pool_ref, 0), (1, s1_ref, 128), (2, s2_ref, 128), (3, s3_ref, 128)):
        at = pl.multiple_of(((z + j) % NZ) * 32, 32)
        ref[pl.ds(base + mine, 32), :] = heads_ref[pl.ds(at, 32), :]
        ref[pl.ds(base + theirs, 32), :] = other_ref[pl.ds(128 + at, 32), :]
        if j:
            ref[:64] = high
            ref[64:128] = low


def up_kernel(sum_ref, r1_ref, r2_ref, r3_ref, local_ref, up_ref, out_ref):
    total = sum_ref[...]
    for ref in (r1_ref, r2_ref, r3_ref):
        total = total + (ref[:64].astype(F32) + ref[64:128].astype(F32))
    shrunk = total.astype(BF16).astype(F32)
    local = local_ref[:1]
    spread = jnp.concatenate(
        [jnp.where(local == g + 1.0, shrunk, 0.0) for g in range(8)], axis=0
    ).astype(BF16)
    out_ref[...] = lax.dot_general(
        spread, up_ref[...], (((0,), (0,)), ((), ())), preferred_element_type=F32
    ).astype(BF16)


def second_kernel(acc_in_ref, x_ref, w_ref, dest_ref, ids_ref, lens_ref, tie_ref, acc_ref, place_ref, bias_ref):
    del tie_ref
    step = pl.program_id(0)

    @pl.when(step == 0)
    def _():
        acc_ref[...] = acc_in_ref[...]
        shard = lax.axis_index("store")
        z = lax.axis_index("ctx") // 2
        place = (dest_ref[:1] == iota((256, 128), 0)).astype(F32)
        place_ref[...] = place.T.astype(BF16)
        row = iota((256, 128), 0)
        block = ((z + NZ - row // 64) % NZ) * 4 + (row % 64) // BLK + shard * 16
        offset = row % BLK
        position = jnp.full((256, 128), 1 << 20, jnp.int32)
        for j in range(ids_ref.shape[0]):
            position = jnp.where(ids_ref[j : j + 1] == block, j * BLK + offset, position)
        bias = jnp.where(position < lens_ref[...], 0.0, -jnp.inf)
        bias_ref[...] = bias.T

    acc_ref[...] += jnp.dot(x_ref[...], w_ref[...], preferred_element_type=F32)


def attend_kernel(acc_ref, returned_ref, place_ref, bias_ref, cos_ref, sin_ref, p0_ref, r1_ref, r2_ref, r3_ref, out_ref):
    update = jnp.dot(place_ref[...], returned_ref[...], preferred_element_type=F32)
    joined = acc_ref[...] + ADAPTER_SCALE * update
    cosine = cos_ref[...]
    sine = sin_ref[...]

    def rope(v):
        return (v * cosine + pltpu.roll(v, HEAD // 2, 1) * sine).astype(BF16)

    key_new = rope(joined[:, 8 * HEAD : 9 * HEAD]).astype(F32)
    value_new = joined[:, 9 * HEAD :].astype(BF16).astype(F32)
    pool = jnp.concatenate([p0_ref[...], r1_ref[128:], r2_ref[128:], r3_ref[128:]], axis=0)
    keys = pool[:, :HEAD]
    values = pool[:, HEAD:]
    bias = bias_ref[...]
    scale = 1.0 / HEAD**0.5
    for g in range(QUERY_PER_KEY):
        query = rope(joined[:, g * HEAD : (g + 1) * HEAD])
        score = lax.dot_general(query, keys, (((1,), (1,)), ((), ())), preferred_element_type=F32)
        score = score * scale + bias
        own = jnp.sum(query.astype(F32) * key_new, axis=1, keepdims=True) * scale
        top = jnp.maximum(jnp.max(score, axis=1, keepdims=True), own)
        prob = jnp.exp(score - top)
        prob_own = jnp.exp(own - top)
        total = jnp.sum(prob, axis=1, keepdims=True) + prob_own
        mixed = jnp.dot(prob.astype(BF16), values, preferred_element_type=F32)
        mixed = mixed + prob_own.astype(BF16).astype(F32) * value_new
        out_ref[:, g * HEAD : (g + 1) * HEAD] = (mixed / total).astype(BF16)


def shapes(*pairs):
    return [jax.ShapeDtypeStruct(s, d) for s, d in pairs]


def call(kernel, out, cost, *args):
    return pl.pallas_call(
        kernel,
        out_shape=out,
        name=kernel.__name__,
        cost_estimate=pl.CostEstimate(flops=cost[0], bytes_accessed=cost[1], transcendentals=0),
        compiler_params=pltpu.CompilerParams(vmem_limit_bytes=16 << 20),
    )(*args)


def whole(shape):
    return pl.BlockSpec(shape, lambda i: (0,) * len(shape))


def body(
    tokens,
    joined_weight,
    down_weight,
    up_weight,
    adapter_per_request,
    adapter_store_slot,
    prefix_block_list,
    prefix_length,
    key_value_pool,
):
    n_store = lax.axis_size("store")
    n_ctx = lax.axis_size("ctx")
    requests, d_model = tokens.shape
    width = down_weight.shape[1]
    columns = joined_weight.shape[2]
    slots = n_store * CAP
    adapters = adapter_per_request.reshape(n_store, requests)
    table = adapter_store_slot.reshape(1, 128)
    weight = joined_weight.reshape(d_model, columns)
    down = down_weight.transpose(0, 2, 1).reshape(-1, width)
    up = up_weight.reshape(-1, columns)
    pool = key_value_pool.reshape(-1, 2 * HEAD)

    outgoing, dest = pl.pallas_call(
        pack_kernel,
        out_shape=shapes(((slots, width), BF16), ((8, 128), jnp.int32)),
        name="pack_kernel",
        in_specs=[
            pl.BlockSpec(memory_space=pltpu.VMEM),
            pl.BlockSpec(memory_space=pltpu.VMEM),
            pl.BlockSpec(memory_space=pl.ANY),
        ],
        scratch_shapes=[pltpu.VMEM((requests, width), BF16), pltpu.SemaphoreType.DMA],
        cost_estimate=pl.CostEstimate(flops=1 << 26, bytes_accessed=1 << 20, transcendentals=0),
        compiler_params=pltpu.CompilerParams(vmem_limit_bytes=16 << 20),
    )(adapters, table, tokens)

    received = lax.all_to_all(
        outgoing.reshape(n_store, CAP, width), "store", split_axis=0, concat_axis=0, tiled=True
    ).reshape(slots, width)

    steps = d_model // BK
    acc, local, heads = pl.pallas_call(
        first_kernel,
        grid=(STEPS_A,),
        out_shape=shapes(((requests, columns), F32), ((8, slots), F32), ((256, 256), BF16)),
        name="first_kernel",
        in_specs=[
            whole(adapters.shape),
            whole(table.shape),
            whole(pool.shape),
            pl.BlockSpec((requests, BK), lambda i: (0, i)),
            pl.BlockSpec((BK, columns), lambda i: (i, 0)),
        ],
        out_specs=[whole((requests, columns)), whole((8, slots)), whole((256, 256))],
        cost_estimate=pl.CostEstimate(
            flops=2 * requests * columns * BK * STEPS_A,
            bytes_accessed=2 * BK * STEPS_A * columns,
            transcendentals=0,
        ),
        compiler_params=pltpu.CompilerParams(vmem_limit_bytes=16 << 20),
    )(adapters, table, pool, tokens, weight)

    part, send = call(
        down_kernel,
        shapes(((64, slots), F32), ((256, 256), BF16)),
        (1 << 28, 1 << 21),
        received,
        down,
        local,
        heads,
    )
    other = lax.ppermute(send, "ctx", [(i, i ^ 1) for i in range(n_ctx)])
    total, pool0, s1, s2, s3 = call(
        middle_kernel,
        shapes(((64, slots), F32), ((64, 256), BF16), *[((192, 256), BF16)] * 3),
        (1 << 16, 1 << 19),
        part,
        heads,
        other,
    )
    r1, r2, r3 = [
        lax.ppermute(s, "ctx", [(i, (i + 2 * j) % n_ctx) for i in range(n_ctx)])
        for j, s in ((1, s1), (2, s2), (3, s3))
    ]
    update = call(
        up_kernel,
        shapes(((slots, columns), BF16))[0],
        (1 << 28, 1 << 21),
        total,
        r1,
        r2,
        r3,
        local,
        up,
    )
    returned = lax.all_to_all(
        update.reshape(n_store, CAP, columns), "store", split_axis=0, concat_axis=0, tiled=True
    ).reshape(slots, columns)

    acc, place, bias = pl.pallas_call(
        second_kernel,
        grid=(steps - STEPS_A,),
        out_shape=shapes(((requests, columns), F32), ((requests, slots), BF16), ((requests, 256), F32)),
        name="second_kernel",
        in_specs=[
            whole((requests, columns)),
            pl.BlockSpec((requests, BK), lambda i: (0, STEPS_A + i)),
            pl.BlockSpec((BK, columns), lambda i: (STEPS_A + i, 0)),
            whole((8, 128)),
            whole((8, 128)),
            whole((1, 128)),
            pl.BlockSpec((16, 128), lambda i: (0, 0)),
        ],
        out_specs=[whole((requests, columns)), whole((requests, slots)), whole((requests, 256))],
        input_output_aliases={0: 0},
        cost_estimate=pl.CostEstimate(
            flops=2 * requests * columns * BK * (steps - STEPS_A),
            bytes_accessed=2 * BK * (steps - STEPS_A) * columns,
            transcendentals=0,
        ),
        compiler_params=pltpu.CompilerParams(vmem_limit_bytes=16 << 20),
    )(acc, tokens, weight, dest, prefix_block_list.T, prefix_length.reshape(1, requests), update)

    frequency = np.power(
        np.float32(ROPE_THETA), -(np.arange(HEAD // 2, dtype=np.float32) * np.float32(2.0 / HEAD))
    ).astype(np.float32)
    angle = prefix_length.astype(F32)[:, None] * jnp.asarray(np.tile(frequency, 2))[None, :]
    cosine = jnp.cos(angle)
    sine = jnp.sin(angle) * jnp.asarray(np.repeat(np.float32([-1.0, 1.0]), HEAD // 2))[None, :]

    out = call(
        attend_kernel,
        shapes(((requests, QUERY_PER_KEY * HEAD), BF16))[0],
        (1 << 28, 1 << 21),
        acc,
        returned,
        place,
        bias,
        cosine,
        sine,
        pool0,
        r1,
        r2,
        r3,
    )
    return out.reshape(requests, 1, QUERY_PER_KEY * HEAD)


def solution(mesh):
    in_specs = (
        P("store", None),
        P(None, "ctx", None),
        P("store", "ctx", None),
        P("store", None, "ctx", None),
        P(),
        P(),
        P("store", None),
        P("store"),
        P(("store", "ctx"), None, None),
    )
    out_specs = P("store", "ctx", None)
    return jax.shard_map(body, mesh=mesh, in_specs=in_specs, out_specs=out_specs, check_vma=False)
```

time: 104 us -> 67 us (0.64)
  blocking collectives: 26.7 us -> 0 us
  local copies, waits for them, and re-layouts: 7.7 us -> 25.4 us
  matrix products: 17.5 us -> 0 us
  between operations: 13.7 us -> 0.21 us
  Pallas kernels: 0 us -> 12.5 us
  waiting for transfers between devices: 16.9 us -> 5.79 us
  starting transfers between devices: 10.9 us -> 20.5 us
  other arithmetic: 10.2 us -> 1.62 us
    psum x1 -> x0, blocking collectives: 26.7 us -> none  [body(): shrunk = lax.psum(shrunk_part, 'ctx').astype(jnp.bfloat16)]
    unnamed x11 -> x52, local copies, waits for them, and re-layouts: 1.89 us -> 25.4 us
    dot_general x6 -> x0, matrix products: 17.5 us -> none  [the longest x1 9.86 us: body(): jnp.dot(tokens, joined_weight.reshape(d_model, head_slice * column_list),...]
    all_to_all x2, waiting for transfers between devices: 16.9 us -> 0.53 us  [the longest x1 0.53 us: body(): lax.all_to_all(outgoing.reshape(n_store, CAP, width), 'store', split_axis...]
    pallas_call x0 -> x7, Pallas kernels: none -> 12.5 us  [the longest x1 3.99 us: body(): pl.pallas_call(second_kernel, grid=(steps - STEPS_A,), out_shape=shapes((...]
    ppermute x0 -> x4, starting transfers between devices: none -> 6.66 us  [the longest x3 6.58 us: body(): lax.ppermute(s, 'ctx', [(i, (i + 2 * j) % n_ctx) for i in range(n_ctx)])]
    ppermute x0 -> x4, waiting for transfers between devices: none -> 5.26 us  [the longest x3 3.92 us: body(): lax.ppermute(s, 'ctx', [(i, (i + 2 * j) % n_ctx) for i in range(n_ctx)])]
    reduce_or x2 -> x0, other arithmetic: 4.46 us -> none  [the longest x1 4.45 us: body(): adapter_hot = jnp.any(adapter_hot, axis=1)]
  transfers between devices with their start and end apart: 3 -> 6, of which waited for: 2 -> 4; matrix products, arithmetic and copies ran while one was open for 29% -> 2% of each run, Pallas kernels for 0% -> 11%
where the time goes in v1:
time: 67 us; the launch traced here: 65.9 us
  local copies, waits for them, and re-layouts  25.4 us (38%)
  starting transfers between devices  20.5 us (31%)
  Pallas kernels  12.5 us (19%)
  waiting for transfers between devices  5.79 us (9%)
  other arithmetic  1.62 us (2%)
    unnamed x52, local copies, waits for them, and re-layouts  25.4 us
    all_to_all x1, starting transfers between devices, body(): lax.all_to_all(outgoing.reshape(n_store, CAP, width), 'store', split_axis...  7.13 us
    all_to_all x1, starting transfers between devices, body(): lax.all_to_all(update.reshape(n_store, CAP, columns), 'store', split_axis...  6.7 us
    ppermute x3, starting transfers between devices, body(): lax.ppermute(s, 'ctx', [(i, (i + 2 * j) % n_ctx) for i in range(n_ctx)])  6.58 us
    pallas_call x1, Pallas kernels, body(): pl.pallas_call(second_kernel, grid=(steps - STEPS_A,), out_shape=shapes((...  3.99 us
    ppermute x3, waiting for transfers between devices, body(): lax.ppermute(s, 'ctx', [(i, (i + 2 * j) % n_ctx) for i in range(n_ctx)])  3.92 us
    pallas_call x4, Pallas kernels, call(): pl.pallas_call(kernel, out_shape=out, name=kernel.__name__, cost_estimate...  3.87 us
    pallas_call x1, Pallas kernels, body(): pl.pallas_call(first_kernel, grid=(STEPS_A,), out_shape=shapes(((requests...  3.29 us
  transfers between devices with their start and end apart: 6, of which 4 were waited for; matrix products, arithmetic and copies ran while one was open for 2% of the time, Pallas kernels for 11%

profile of v1, /device:TPU:0, one launch (start us, length us, event | category | flops | bytes accessed | tf_op | source)
XLA Modules:
  0.0 65.9 jit_solution(6431397765610844121)
XLA Ops:
  0.0 1.6 %copy-done.2 = bf16[128,8192]{1,0:T(8,128)(2,1)S(1)} copy-done((bf16[128,8192]{1,0:T(8,128)(2,1)S(1)}, bf16[128,8192]{1,0:T(8,128)(2,1)}, u32[]{:S(2)}) %copy-start.2) | copy-done | bytes 2097176
  1.6 0.7 %copy-done.17 = s32[2048]{0:T(1024)S(1)} copy-done((s32[2048]{0:T(1024)S(1)}, s32[2048]{0:T(1024)}, u32[]{:S(2)}) %copy-start.17) | copy-done | bytes 8216
  3.0 1.3 %pack_kernel.1 = (bf16[256,1024]{1,0:T(8,128)(2,1)}, s32[8,128]{1,0:T(8,128)S(1)}) custom-call(s32[16,128]{1,0:T(8,128)S(1)} %bitcast.22, s32[1,128]{1,0:T(1,128)S(1)} %bitcast.25, bf16[128,8192]{1,0:T(8,128)(2,1)S(1)} %copy-done.2), custom_call_target="tpu_custom_call" | custom-call | flops 67108864 | bytes 1048576 | tf_op jit(solution)/shard_map/pack_kernel/pallas_call | solution.py:233
  4.3 7.1 %all-to-all-start = ((bf16[16,16,1024]{2,1,0:T(8,128)(2,1)}), bf16[16,16,1024]{2,1,0:T(8,128)(2,1)S(1)}, u32[]{:S(2)}, u32[]{:S(2)}) async-start(bf16[16,16,1024]{2,1,0:T(8,128)(2,1)} %bitcast.6), calls=%async_computation | async-start | bytes 1048576 | tf_op jit(solution)/shard_map/all_to_all | solution.py:247
  11.5 7.0 %copy-done = bf16[8192,1,1280]{2,0,1:T(8,128)(2,1)S(1)} copy-done((bf16[8192,1,1280]{2,0,1:T(8,128)(2,1)S(1)}, bf16[8192,1,1280]{2,0,1:T(8,128)(2,1)}, u32[]{:S(2)}) %copy-start) | copy-done | bytes 20971544
  19.1 3.3 %first_kernel.1 = (f32[128,1280]{1,0:T(8,128)S(1)}, f32[8,256]{1,0:T(8,128)S(1)}, bf16[256,256]{1,0:T(8,128)(2,1)S(1)}) custom-call(s32[16,128]{1,0:T(8,128)S(1)} %bitcast.23, s32[1,128]{1,0:T(1,128)S(1)} %bitcast.26, bf16[256,256]{1,0:T(8,128)(2,1)S(1)} %bitcast.21, bf16[128,8192]{1,0:T(8,128)(2,1)S(1)} %copy-done.3, bf16[8192,1280]{1,0:T(8,128)(2,1)S(1)} %bitcast.15), custom_call_target="tpu_custom_call" | custom-call | flops 1342177280 | bytes 10485760 | tf_op jit(solution)/shard_map/first_kernel/pallas_call | solution.py:252
  22.9 1.3 %copy-done.5 = bf16[8,1024,64]{1,2,0:T(8,128)(2,1)S(1)} copy-done((bf16[8,1024,64]{1,2,0:T(8,128)(2,1)S(1)}, bf16[8,1024,64]{1,2,0:T(8,128)(2,1)}, u32[]{:S(2)}) %copy-start.5) | copy-done | bytes 1048600
  24.9 1.3 %collective-permute-done.other_ref = bf16[256,256]{1,0:T(8,128)(2,1)S(1)} collective-permute-done((bf16[256,256]{1,0:T(8,128)(2,1)S(1)}, bf16[256,256]{1,0:T(8,128)(2,1)S(1)}, u32[]{:S(2)}, u32[]{:S(2)}) %collective-permute-start) | collective-permute-done | bytes 131104 | tf_op jit(solution)/shard_map/ppermute | solution.py:282
  26.3 2.0 %collective-permute-start.1 = (bf16[192,256]{1,0:T(8,128)(2,1)S(1)}, bf16[192,256]{1,0:T(8,128)(2,1)S(1)}, u32[]{:S(2)}, u32[]{:S(2)}) collective-permute-start(bf16[192,256]{1,0:T(8,128)(2,1)S(1)} %get-tuple-element.28), channel_id=1, source_target_pairs={{0,2},{1,3},{2,4},{3,5},{4,6},{5,7},{6,0},{7,1},{8,10},{9,11},{10,... | collective-permute-start | bytes 294920 | tf_op jit(solution)/shard_map/ppermute | solution.py:292
  28.2 3.6 %collective-permute-start.2 = (bf16[192,256]{1,0:T(8,128)(2,1)S(1)}, bf16[192,256]{1,0:T(8,128)(2,1)S(1)}, u32[]{:S(2)}, u32[]{:S(2)}) collective-permute-start(bf16[192,256]{1,0:T(8,128)(2,1)S(1)} %get-tuple-element.29), channel_id=1, source_target_pairs={{0,4},{1,5},{2,6},{3,7},{4,0},{5,1},{6,2},{7,3},{8,12},{9,13},{10,... | collective-permute-start | bytes 294920 | tf_op jit(solution)/shard_map/ppermute | solution.py:292
  31.8 1.0 %collective-permute-start.3 = (bf16[192,256]{1,0:T(8,128)(2,1)S(1)}, bf16[192,256]{1,0:T(8,128)(2,1)S(1)}, u32[]{:S(2)}, u32[]{:S(2)}) collective-permute-start(bf16[192,256]{1,0:T(8,128)(2,1)S(1)} %get-tuple-element.30), channel_id=1, source_target_pairs={{0,6},{1,7},{2,0},{3,1},{4,2},{5,3},{6,4},{7,5},{8,14},{9,15},{10,... | collective-permute-start | bytes 294920 | tf_op jit(solution)/shard_map/ppermute | solution.py:292
  33.5 3.3 %collective-permute-done.2.r2_ref = bf16[192,256]{1,0:T(8,128)(2,1)S(1)} collective-permute-done((bf16[192,256]{1,0:T(8,128)(2,1)S(1)}, bf16[192,256]{1,0:T(8,128)(2,1)S(1)}, u32[]{:S(2)}, u32[]{:S(2)}) %collective-permute-start.2) | collective-permute-done | bytes 98336 | tf_op jit(solution)/shard_map/ppermute | solution.py:292
  36.8 1.4 %up_kernel.1.tie_ref = bf16[256,1280]{1,0:T(8,128)(2,1)} custom-call(f32[64,256]{1,0:T(8,128)S(1)} %get-tuple-element.27.sum_ref, bf16[192,256]{1,0:T(8,128)(2,1)S(1)} %collective-permute-done.1.r1_ref, bf16[192,256]{1,0:T(8,128)(2,1)S(1)} %collective-permute-done.2.r2_ref, bf16[192,256]{1,0:T(8,128)(2,1)S(1)} %collective-permute-done.3.r3_ref, ...), custom_call_target="tpu_custom_call" | custom-call | flops 268435456 | bytes 2097152 | tf_op jit(solution)/shard_map/up_kernel/pallas_call | solution.py:196
  38.2 6.7 %all-to-all-start.1 = ((bf16[16,16,1280]{2,1,0:T(8,128)(2,1)}), bf16[16,16,1280]{2,1,0:T(8,128)(2,1)S(1)}, u32[]{:S(2)}, u32[]{:S(2)}) async-start(bf16[16,16,1280]{2,1,0:T(8,128)(2,1)} %bitcast.11), calls=%async_computation.1 | async-start | bytes 1310720 | tf_op jit(solution)/shard_map/all_to_all | solution.py:306
  44.9 1.6 %fusion = (f32[128,128]{1,0:T(8,128)}, f32[128,128]{1,0:T(8,128)}) fusion(f32[128]{0:T(128)} %constant.5.clone, f32[128]{0:T(128)S(1)} %copy-done.25, f32[128]{0:T(128)S(1)} %convert_element_type.3), kind=kLoop, calls=%fused_computation.2 | loop fusion | flops 32768 | bytes 132608 | tf_op jit(solution)/shard_map/mul | solution.py:339
  46.6 7.0 %copy-done.1 = bf16[8192,1,1280]{2,0,1:T(8,128)(2,1)S(1)} copy-done((bf16[8192,1,1280]{2,0,1:T(8,128)(2,1)S(1)}, bf16[8192,1,1280]{2,0,1:T(8,128)(2,1)}, u32[]{:S(2)}) %copy-start.1) | copy-done | bytes 20971544
  53.5 4.0 %second_kernel.1 = (f32[128,1280]{1,0:T(8,128)S(1)}, bf16[128,256]{1,0:T(8,128)(2,1)S(1)}, f32[128,256]{1,0:T(8,128)S(1)}) custom-call(f32[128,1280]{1,0:T(8,128)S(1)} %get-tuple-element.20.acc_in_ref, bf16[128,8192]{1,0:T(8,128)(2,1)S(1)} %copy-done.3, bf16[8192,1280]{1,0:T(8,128)(2,1)S(1)} %bitcast.16, ...), custom_call_target="tpu_custom_call", output_to_operand_aliasing={{0}: (0, {})} | custom-call | flops 1342177280 | bytes 10485760 | tf_op jit(solution)/shard_map/second_kernel/pallas_call | solution.py:310
  58.8 0.9 %copy-done.7 = bf16[192,256]{1,0:T(8,128)(2,1)S(1)} copy-done((bf16[192,256]{1,0:T(8,128)(2,1)S(1)}, bf16[192,256]{1,0:T(8,128)(2,1)}, u32[]{:S(2)}) %copy-start.7) | copy-done | bytes 98328
  59.7 0.9 %copy-done.9 = bf16[192,256]{1,0:T(8,128)(2,1)S(1)} copy-done((bf16[192,256]{1,0:T(8,128)(2,1)S(1)}, bf16[192,256]{1,0:T(8,128)(2,1)}, u32[]{:S(2)}) %copy-start.9) | copy-done | bytes 98328
  60.6 0.8 %copy-done.10 = f32[128,128]{1,0:T(8,128)S(1)} copy-done((f32[128,128]{1,0:T(8,128)S(1)}, f32[128,128]{1,0:T(8,128)}, u32[]{:S(2)}) %copy-start.10) | copy-done | bytes 65560
  61.4 0.8 %copy-done.11 = f32[128,128]{1,0:T(8,128)S(1)} copy-done((f32[128,128]{1,0:T(8,128)S(1)}, f32[128,128]{1,0:T(8,128)}, u32[]{:S(2)}) %copy-start.11) | copy-done | bytes 65560
  62.3 0.9 %copy-done.14 = f32[128,256]{1,0:T(8,128)S(1)} copy-done((f32[128,256]{1,0:T(8,128)S(1)}, f32[128,256]{1,0:T(8,128)}, u32[]{:S(2)}) %copy-start.14) | copy-done | bytes 131096
  63.2 0.8 %copy-done.16 = bf16[128,256]{1,0:T(8,128)(2,1)S(1)} copy-done((bf16[128,256]{1,0:T(8,128)(2,1)S(1)}, bf16[128,256]{1,0:T(8,128)(2,1)}, u32[]{:S(2)}) %copy-start.16) | copy-done | bytes 65560
  64.0 1.9 %attend_kernel.1 = bf16[128,1024]{1,0:T(8,128)(2,1)} custom-call(f32[128,1280]{1,0:T(8,128)S(1)} %get-tuple-element.31.acc_ref, bf16[256,1280]{1,0:T(8,128)(2,1)S(1)} %bitcast.17, bf16[128,256]{1,0:T(8,128)(2,1)S(1)} %copy-done.16, f32[128,256]{1,0:T(8,128)S(1)} %copy-done.14, f32[128,128]{1,0:T(8,128)S(1)} %copy-done.11, f32[128,128]{1,0:T(8,128)S(1)} %copy-done.10, ...), custom_call_target="tpu_custom_call" | custom-call | flops 268435456 | bytes 2097152 | tf_op jit(solution)/shard_map/attend_kernel/pallas_call | solution.py:196
  (49 shorter events, 4.4 us)
Async XLA Ops:
  0.0 1.6 %copy-start.2 = (bf16[128,8192]{1,0:T(8,128)(2,1)S(1)}, bf16[128,8192]{1,0:T(8,128)(2,1)}, u32[]{:S(2)}) copy-start(bf16[128,8192]{1,0:T(8,128)(2,1)} %x_ref.3) | copy-start | bytes 6291460
  2.9 8.5 %copy-start.3 = (bf16[128,8192]{1,0:T(8,128)(2,1)S(1)}, bf16[128,8192]{1,0:T(8,128)(2,1)}, u32[]{:S(2)}) copy-start(bf16[128,8192]{1,0:T(8,128)(2,1)} %x_ref.3) | copy-start | bytes 6291460
  2.9 8.5 %copy-start.12 = (bf16[32,8,256]{2,1,0:T(8,128)(2,1)S(1)}, bf16[32,8,256]{2,1,0:T(8,128)(2,1)}, u32[]{:S(2)}) copy-start(bf16[32,8,256]{2,1,0:T(8,128)(2,1)} %param.19) | copy-start | bytes 393220
  2.9 8.5 %copy-start.18 = (s32[2048]{0:T(1024)S(1)}, s32[2048]{0:T(1024)}, u32[]{:S(2)}) copy-start(s32[2048]{0:T(1024)} %param.15) | copy-start | bytes 24580
  4.3 7.2 %copy-start.20 = (s32[8,128]{1,0:T(8,128)}, s32[8,128]{1,0:T(8,128)S(1)}, u32[]{:S(2)}) copy-start(s32[8,128]{1,0:T(8,128)S(1)} %get-tuple-element.21.dest_ref) | copy-start | bytes 12292
  4.3 18.6 %all-to-all-start = ((bf16[16,16,1024]{2,1,0:T(8,128)(2,1)}), bf16[16,16,1024]{2,1,0:T(8,128)(2,1)S(1)}, u32[]{:S(2)}, u32[]{:S(2)}) async-start(bf16[16,16,1024]{2,1,0:T(8,128)(2,1)} %bitcast.6), calls=%async_computation | async-start | bytes 1048576 | tf_op jit(solution)/shard_map/all_to_all | solution.py:247
  11.5 7.0 %copy-start = (bf16[8192,1,1280]{2,0,1:T(8,128)(2,1)S(1)}, bf16[8192,1,1280]{2,0,1:T(8,128)(2,1)}, u32[]{:S(2)}) copy-start(bf16[8192,1,1280]{2,0,1:T(8,128)(2,1)} %param.12) | copy-start | bytes 62914564
  22.9 13.9 %copy-start.4 = (bf16[8,64,1,1280]{3,1,2,0:T(8,128)(2,1)S(1)}, bf16[8,64,1,1280]{3,1,2,0:T(8,128)(2,1)}, u32[]{:S(2)}) copy-start(bf16[8,64,1,1280]{3,1,2,0:T(8,128)(2,1)} %param.14) | copy-start | bytes 3932164
  22.9 1.3 %copy-start.5 = (bf16[8,1024,64]{1,2,0:T(8,128)(2,1)S(1)}, bf16[8,1024,64]{1,2,0:T(8,128)(2,1)}, u32[]{:S(2)}) copy-start(bf16[8,1024,64]{1,2,0:T(8,128)(2,1)} %param.13) | copy-start | bytes 3145732
  24.7 20.2 %copy-start.24 = (s32[128]{0:T(128)S(1)}, s32[128]{0:T(128)}, u32[]{:S(2)}) copy-start(s32[128]{0:T(128)} %param.18) | copy-start | bytes 1540
  24.8 20.2 %copy-start.25 = (f32[128]{0:T(128)S(1)}, f32[128]{0:T(128)}, u32[]{:S(2)}) copy-start(f32[128]{0:T(128)} %constant.4.clone) | copy-start | bytes 1540
  24.8 21.8 %copy-start.19 = (s32[128,8]{0,1:T(8,128)S(1)}, s32[128,8]{0,1:T(8,128)}, u32[]{:S(2)}) copy-start(s32[128,8]{0,1:T(8,128)} %param.17) | copy-start | bytes 12292
  24.8 21.8 %copy-start.21 = (s32[8,128]{1,0:T(8,128)S(1)}, s32[8,128]{1,0:T(8,128)}, u32[]{:S(2)}) copy-start(s32[8,128]{1,0:T(8,128)} %copy-done.20) | copy-start | bytes 12292
  24.8 1.4 %collective-permute-start = (bf16[256,256]{1,0:T(8,128)(2,1)S(1)}, bf16[256,256]{1,0:T(8,128)(2,1)S(1)}, u32[]{:S(2)}, u32[]{:S(2)}) collective-permute-start(bf16[256,256]{1,0:T(8,128)(2,1)S(1)} %get-tuple-element.26), channel_id=1, source_target_pairs={{0,1},{1,0},{2,3},{3,2},{4,5},{5,4},{6,7},{7,6},{8,9},{9,8},{10,11... | collective-permute-start | bytes 393224 | tf_op jit(solution)/shard_map/ppermute | solution.py:282
  26.3 7.2 %collective-permute-start.1 = (bf16[192,256]{1,0:T(8,128)(2,1)S(1)}, bf16[192,256]{1,0:T(8,128)(2,1)S(1)}, u32[]{:S(2)}, u32[]{:S(2)}) collective-permute-start(bf16[192,256]{1,0:T(8,128)(2,1)S(1)} %get-tuple-element.28), channel_id=1, source_target_pairs={{0,2},{1,3},{2,4},{3,5},{4,6},{5,7},{6,0},{7,1},{8,10},{9,11},{10,... | collective-permute-start | bytes 294920 | tf_op jit(solution)/shard_map/ppermute | solution.py:292
  28.2 8.5 %collective-permute-start.2 = (bf16[192,256]{1,0:T(8,128)(2,1)S(1)}, bf16[192,256]{1,0:T(8,128)(2,1)S(1)}, u32[]{:S(2)}, u32[]{:S(2)}) collective-permute-start(bf16[192,256]{1,0:T(8,128)(2,1)S(1)} %get-tuple-element.29), channel_id=1, source_target_pairs={{0,4},{1,5},{2,6},{3,7},{4,0},{5,1},{6,2},{7,3},{8,12},{9,13},{10,... | collective-permute-start | bytes 294920 | tf_op jit(solution)/shard_map/ppermute | solution.py:292
  31.8 4.9 %collective-permute-start.3 = (bf16[192,256]{1,0:T(8,128)(2,1)S(1)}, bf16[192,256]{1,0:T(8,128)(2,1)S(1)}, u32[]{:S(2)}, u32[]{:S(2)}) collective-permute-start(bf16[192,256]{1,0:T(8,128)(2,1)S(1)} %get-tuple-element.30), channel_id=1, source_target_pairs={{0,6},{1,7},{2,0},{3,1},{4,2},{5,3},{6,4},{7,5},{8,14},{9,15},{10,... | collective-permute-start | bytes 294920 | tf_op jit(solution)/shard_map/ppermute | solution.py:292
  36.8 1.4 %copy-start.6 = (bf16[192,256]{1,0:T(8,128)(2,1)}, bf16[192,256]{1,0:T(8,128)(2,1)S(1)}, u32[]{:S(2)}) copy-start(bf16[192,256]{1,0:T(8,128)(2,1)S(1)} %collective-permute-done.2.r2_ref) | copy-start | bytes 294916
  36.8 1.4 %copy-start.8 = (bf16[192,256]{1,0:T(8,128)(2,1)}, bf16[192,256]{1,0:T(8,128)(2,1)S(1)}, u32[]{:S(2)}) copy-start(bf16[192,256]{1,0:T(8,128)(2,1)S(1)} %collective-permute-done.3.r3_ref) | copy-start | bytes 294916
  38.2 20.6 %all-to-all-start.1 = ((bf16[16,16,1280]{2,1,0:T(8,128)(2,1)}), bf16[16,16,1280]{2,1,0:T(8,128)(2,1)S(1)}, u32[]{:S(2)}, u32[]{:S(2)}) async-start(bf16[16,16,1280]{2,1,0:T(8,128)(2,1)} %bitcast.11), calls=%async_computation.1 | async-start | bytes 1310720 | tf_op jit(solution)/shard_map/all_to_all | solution.py:306
  46.6 7.0 %copy-start.1 = (bf16[8192,1,1280]{2,0,1:T(8,128)(2,1)S(1)}, bf16[8192,1,1280]{2,0,1:T(8,128)(2,1)}, u32[]{:S(2)}) copy-start(bf16[8192,1,1280]{2,0,1:T(8,128)(2,1)} %param.12) | copy-start | bytes 62914564
  58.8 0.9 %copy-start.7 = (bf16[192,256]{1,0:T(8,128)(2,1)S(1)}, bf16[192,256]{1,0:T(8,128)(2,1)}, u32[]{:S(2)}) copy-start(bf16[192,256]{1,0:T(8,128)(2,1)} %copy-done.6) | copy-start | bytes 294916
  59.7 0.9 %copy-start.9 = (bf16[192,256]{1,0:T(8,128)(2,1)S(1)}, bf16[192,256]{1,0:T(8,128)(2,1)}, u32[]{:S(2)}) copy-start(bf16[192,256]{1,0:T(8,128)(2,1)} %copy-done.8) | copy-start | bytes 294916
  62.3 0.9 %copy-start.14 = (f32[128,256]{1,0:T(8,128)S(1)}, f32[128,256]{1,0:T(8,128)}, u32[]{:S(2)}) copy-start(f32[128,256]{1,0:T(8,128)} %copy-done.13) | copy-start | bytes 393220
  (8 other events, 5.8 us)

commit v2 on v1

v2 whole, which is shorter than its diff:
```python
import jax
import jax.numpy as jnp
import numpy as np
from jax import lax
from jax.experimental import pallas as pl
from jax.experimental.pallas import tpu as pltpu
from jax.sharding import PartitionSpec as P

QUERY_PER_KEY = 8
HEAD = 128
CAP = 16
BLK = 16
NZ = 4
ROPE_THETA = 500000.0
ADAPTER_SCALE = 2.0
BK = 512
AHEAD = 4
STEPS_A = 8

F32 = jnp.float32
BF16 = jnp.bfloat16


def iota(shape, dim):
    return lax.broadcasted_iota(jnp.int32, shape, dim)


def before():
    return (iota((128, 128), 0) < iota((128, 128), 1)).astype(BF16)


def pack_kernel(adapter_hbm, table_hbm, tokens_hbm, out_ref, dest_ref, adapter_ref, table_ref, x_ref, sems):
    shard = lax.axis_index("store")
    width = x_ref.shape[1]
    start = pl.multiple_of(lax.axis_index("ctx") * width, 128)
    copies = [
        pltpu.make_async_copy(adapter_hbm, adapter_ref, sems.at[0]),
        pltpu.make_async_copy(table_hbm, table_ref, sems.at[1]),
        pltpu.make_async_copy(tokens_hbm.at[:, pl.ds(start, width)], x_ref, sems.at[2]),
    ]
    for copy in copies:
        copy.start()
    copies[0].wait()
    copies[1].wait()
    shards = adapter_ref.shape[0]
    mine = jnp.broadcast_to(adapter_ref[pl.ds(shard, 1), :], (8, 128))
    table = jnp.broadcast_to(table_ref[...], (8, 128))
    slot = jnp.take_along_axis(table, mine, axis=1)[:1]
    owner = slot // 8
    hot = (owner == iota((shards, 128), 0)).astype(F32)
    counted = jnp.dot(hot.astype(BF16), before(), preferred_element_type=F32)
    rank = jnp.sum(hot * counted, axis=0, keepdims=True).astype(jnp.int32)
    dest = owner * CAP + rank
    dest_ref[...] = jnp.broadcast_to(dest, dest_ref.shape)
    place = (dest == iota((shards * CAP, 128), 0)).astype(F32).astype(BF16)
    copies[2].wait()
    out_ref[...] = jnp.dot(place, x_ref[...], preferred_element_type=F32).astype(BF16)


def stream(x_hbm, w_hbm, x_ref, w_ref, sems, first, steps):
    copies = []
    for i in range(steps):
        here = pl.ds(i * BK, BK)
        there = pl.ds((first + i) * BK, BK)
        copies.append(
            (
                pltpu.make_async_copy(x_hbm.at[:, there], x_ref.at[:, here], sems.at[i, 0]),
                pltpu.make_async_copy(w_hbm.at[there, :], w_ref.at[here, :], sems.at[i, 1]),
            )
        )
    for pair in copies[:AHEAD]:
        for copy in pair:
            copy.start()
    return copies


def multiply(copies, acc_ref, x_ref, w_ref):
    for i, pair in enumerate(copies):
        for copy in pair:
            copy.wait()
        if i + AHEAD < len(copies):
            for copy in copies[i + AHEAD]:
                copy.start()
        rows = slice(i * BK, (i + 1) * BK)
        acc_ref[...] += jnp.dot(x_ref[:, rows], w_ref[rows, :], preferred_element_type=F32)


def first_kernel(
    adapter_hbm, table_hbm, pool_hbm, x_hbm, w_hbm,
    acc_ref, local_ref, heads_ref,
    adapter_ref, table_ref, pool_ref, x_ref, w_ref, sems, more,
):
    small = [
        pltpu.make_async_copy(adapter_hbm, adapter_ref, more.at[0]),
        pltpu.make_async_copy(table_hbm, table_ref, more.at[1]),
        pltpu.make_async_copy(pool_hbm, pool_ref, more.at[2]),
    ]
    for copy in small:
        copy.start()
    copies = stream(x_hbm, w_hbm, x_ref, w_ref, sems, 0, STEPS_A)
    for copy in small:
        copy.wait()
    shard = lax.axis_index("store")
    core = lax.axis_index("ctx") % 2
    shards = adapter_ref.shape[0]
    table = jnp.broadcast_to(table_ref[...], (shards, 128))
    slot = jnp.take_along_axis(table, adapter_ref[...], axis=1)
    sent = (slot // 8 == shard).astype(F32)
    rank = jnp.dot(sent.astype(BF16), before(), preferred_element_type=F32)
    rank = jnp.where(sent > 0, rank, -1.0)
    value = (slot % 8 + 1).astype(F32)
    position = iota((CAP, 128), 0).astype(F32)
    rows = [jnp.where(rank[h : h + 1] == position, value[h : h + 1], 0.0) for h in range(shards)]
    column = jnp.sum(jnp.concatenate(rows, axis=0), axis=1, keepdims=True)
    local_ref[...] = jnp.broadcast_to(column, local_ref.shape)
    row = iota((256, 256), 0)
    parity = jnp.where(row < 128, core, 1 - core)
    source = (row % 32) * 8 + ((row // 32) % NZ) * 2 + parity
    select = (source == iota((256, 256), 1)).astype(F32).astype(BF16)
    heads_ref[...] = jnp.dot(select, pool_ref[...], preferred_element_type=F32).astype(BF16)
    acc_ref[...] = jnp.zeros_like(acc_ref)
    multiply(copies, acc_ref, x_ref, w_ref)


def split_sum(x):
    high = x.astype(BF16).astype(F32)
    return jnp.where(iota(x.shape, 1) < 64, high, x - high).astype(BF16)


def join_sum(x):
    x = x.astype(F32)
    return x + pltpu.roll(x, 64, 1)


def down_kernel(received_ref, down_ref, local_ref, heads_ref, part_ref, send_ref):
    every = lax.dot_general(
        received_ref[...], down_ref[...], (((1,), (1,)), ((), ())), preferred_element_type=F32
    )
    local = local_ref[...]
    half = (iota(local.shape, 1) // 64).astype(F32)
    part = jnp.zeros(local.shape, F32)
    for m in range(4):
        part = part + jnp.where(local == 2.0 * m + 1.0 + half, every[:, m * 128 : (m + 1) * 128], 0.0)
    part = part + pltpu.roll(part, 64, 1)
    part_ref[...] = part
    send_ref[:256] = split_sum(part)
    send_ref[256:384] = heads_ref[128:, :HEAD]
    send_ref[384:] = heads_ref[128:, HEAD:]


def middle_kernel(part_ref, heads_ref, other_ref, sum_ref, pool_ref, s1_ref, s2_ref, s3_ref):
    member = lax.axis_index("ctx")
    core = member % 2
    z = member // 2
    total = part_ref[...] + join_sum(other_ref[:256])
    sum_ref[...] = total
    both = split_sum(total)
    mine = pl.multiple_of(core * 32, 32)
    theirs = pl.multiple_of((1 - core) * 32, 32)
    for j, ref, base in ((0, pool_ref, 0), (1, s1_ref, 256), (2, s2_ref, 256), (3, s3_ref, 256)):
        at = pl.multiple_of(((z + j) % NZ) * 32, 32)
        for side in range(2):
            to = base + 64 * side
            columns = slice(side * HEAD, (side + 1) * HEAD)
            ref[pl.ds(to + mine, 32), :] = heads_ref[pl.ds(at, 32), columns]
            ref[pl.ds(to + theirs, 32), :] = other_ref[pl.ds(256 + 128 * side + at, 32), :]
        if j:
            ref[:256] = both


def up_kernel(sum_ref, r1_ref, r2_ref, r3_ref, local_ref, up_ref, out_ref):
    total = sum_ref[...]
    for ref in (r1_ref, r2_ref, r3_ref):
        total = total + join_sum(ref[:256])
    shrunk = total.astype(BF16).astype(F32)
    local = local_ref[...]
    half = (iota(local.shape, 1) // 64).astype(F32)
    spread = jnp.concatenate(
        [jnp.where(local == 2.0 * m + 1.0 + half, shrunk, 0.0).astype(BF16) for m in range(4)], axis=1
    )
    out_ref[...] = jnp.dot(spread, up_ref[...], preferred_element_type=F32).astype(BF16)


ACC = slice(0, 1280)
BIAS = slice(1280, 1536)
COS = slice(1536, 1664)
SIN = slice(1664, 1792)
DEST = slice(1792, 1920)
POOL = 1920
AUX = 2432


def second_kernel(
    acc_hbm, dest_ref, ids_hbm, lens_hbm, cos_ref, sin_ref, x_hbm, w_hbm, p0_ref, r1_ref, r2_ref, r3_ref, tie_ref,
    aux_ref,
    ids_ref, lens_ref, acc_ref, x_ref, w_ref, sems, more,
):
    del tie_ref
    small = [
        pltpu.make_async_copy(ids_hbm, ids_ref, more.at[0]),
        pltpu.make_async_copy(lens_hbm, lens_ref, more.at[1]),
        pltpu.make_async_copy(acc_hbm, acc_ref, more.at[2]),
    ]
    for copy in small:
        copy.start()
    copies = stream(x_hbm, w_hbm, x_ref, w_ref, sems, STEPS_A, sems.shape[0])
    aux_ref[:, DEST] = jnp.broadcast_to(dest_ref[:1].astype(F32), (128, 128)).T
    cosine = cos_ref[...]
    sine = sin_ref[...]
    aux_ref[:, COS] = jnp.concatenate([cosine, cosine], axis=1)
    aux_ref[:, SIN] = jnp.concatenate([-sine, sine], axis=1)
    for i, (ref, at) in enumerate(((p0_ref, 0), (r1_ref, 256), (r2_ref, 256), (r3_ref, 256))):
        rows = slice(64 * (i % 2), 64 * (i % 2) + 64)
        column = POOL + 256 * (i // 2)
        aux_ref[rows, column : column + 128] = ref[at : at + 64].astype(F32)
        aux_ref[rows, column + 128 : column + 256] = ref[at + 64 : at + 128].astype(F32)
    small[0].wait()
    small[1].wait()
    shard = lax.axis_index("store")
    z = lax.axis_index("ctx") // 2
    row = iota((256, 128), 0)
    block = ((z + NZ - row // 64) % NZ) * 4 + (row % 64) // BLK + shard * 16
    offset = row % BLK
    position = jnp.full((256, 128), 1 << 20, jnp.int32)
    for j in range(ids_ref.shape[0]):
        position = jnp.where(ids_ref[j : j + 1] == block, j * BLK + offset, position)
    aux_ref[:, BIAS] = jnp.where(position < lens_ref[...], 0.0, -jnp.inf).T
    small[2].wait()
    multiply(copies, acc_ref, x_ref, w_ref)
    aux_ref[:, ACC] = acc_ref[...]


def attend_kernel(aux_ref, returned_ref, out_ref):
    slots = returned_ref.shape[0]
    dest = aux_ref[:, DEST]
    dest = jnp.concatenate([dest] * (slots // 128), axis=1)
    place = (dest == iota(dest.shape, 1).astype(F32)).astype(F32).astype(BF16)
    update = jnp.dot(place, returned_ref[...], preferred_element_type=F32)
    joined = aux_ref[:, ACC] + ADAPTER_SCALE * update
    cosine = aux_ref[:, COS]
    sine = aux_ref[:, SIN]

    def rope(v):
        return (v * cosine + pltpu.roll(v, HEAD // 2, 1) * sine).astype(BF16)

    key_new = rope(joined[:, 8 * HEAD : 9 * HEAD]).astype(F32)
    value_new = joined[:, 9 * HEAD :].astype(BF16).astype(F32)
    keys = jnp.concatenate([aux_ref[:, POOL + c : POOL + c + 128] for c in (0, 256)], axis=0).astype(BF16)
    values = jnp.concatenate([aux_ref[:, POOL + c : POOL + c + 128] for c in (128, 384)], axis=0).astype(BF16)
    bias = aux_ref[:, BIAS]
    scale = 1.0 / HEAD**0.5
    for g in range(QUERY_PER_KEY):
        query = rope(joined[:, g * HEAD : (g + 1) * HEAD])
        score = lax.dot_general(query, keys, (((1,), (1,)), ((), ())), preferred_element_type=F32)
        score = score * scale + bias
        own = jnp.sum(query.astype(F32) * key_new, axis=1, keepdims=True) * scale
        top = jnp.maximum(jnp.max(score, axis=1, keepdims=True), own)
        prob = jnp.exp(score - top)
        prob_own = jnp.exp(own - top)
        total = jnp.sum(prob, axis=1, keepdims=True) + prob_own
        mixed = jnp.dot(prob.astype(BF16), values, preferred_element_type=F32)
        mixed = mixed + prob_own.astype(BF16).astype(F32) * value_new
        out_ref[:, g * HEAD : (g + 1) * HEAD] = (mixed / total).astype(BF16)


def shapes(*pairs):
    return [jax.ShapeDtypeStruct(s, d) for s, d in pairs]


HBM = pl.BlockSpec(memory_space=pltpu.HBM)
VMEM = pl.BlockSpec(memory_space=pltpu.VMEM)


def call(kernel, out, cost, *args, ins=None, scratch=(), vmem=8):
    return pl.pallas_call(
        kernel,
        out_shape=out,
        name=kernel.__name__,
        in_specs=ins or [VMEM] * len(args),
        scratch_shapes=scratch,
        cost_estimate=pl.CostEstimate(flops=int(cost[0]*1), bytes_accessed=int(cost[1]*1), transcendentals=0),
        compiler_params=pltpu.CompilerParams(vmem_limit_bytes=vmem << 20),
    )(*args)


def body(
    tokens,
    joined_weight,
    down_weight,
    up_weight,
    adapter_per_request,
    adapter_store_slot,
    prefix_block_list,
    prefix_length,
    key_value_pool,
):
    n_store = lax.axis_size("store")
    n_ctx = lax.axis_size("ctx")
    requests, d_model = tokens.shape
    width = down_weight.shape[1]
    columns = joined_weight.shape[2]
    slots = n_store * CAP
    adapters = adapter_per_request.reshape(n_store, requests)
    table = adapter_store_slot.reshape(1, 128)
    weight = joined_weight.reshape(d_model, columns)
    down = down_weight.transpose(0, 2, 1).reshape(-1, width)
    up = up_weight.reshape(-1, columns)
    pool = key_value_pool.reshape(-1, 2 * HEAD)
    tokens, weight, adapters, table, pool = [
        pltpu.with_memory_space_constraint(a, pltpu.HBM) for a in (tokens, weight, adapters, table, pool)
    ]
    small = [pltpu.VMEM(adapters.shape, jnp.int32), pltpu.VMEM(table.shape, jnp.int32)]

    outgoing, dest = call(
        pack_kernel,
        shapes(((slots, width), BF16), ((8, 128), jnp.int32)),
        (1 << 26, 1 << 20),
        adapters,
        table,
        tokens,
        ins=[HBM] * 3,
        vmem=8,
        scratch=[*small, pltpu.VMEM((requests, width), BF16), pltpu.SemaphoreType.DMA((3,))],
    )
    received = lax.all_to_all(
        outgoing.reshape(n_store, CAP, width), "store", split_axis=0, concat_axis=0, tiled=True
    ).reshape(slots, width)

    def parts(steps):
        return [
            pltpu.VMEM((requests, steps * BK), BF16),
            pltpu.VMEM((steps * BK, columns), BF16),
            pltpu.SemaphoreType.DMA((steps, 2)),
            pltpu.SemaphoreType.DMA((4,)),
        ]

    def cost(steps):
        return (2 * requests * columns * BK * steps, 2 * BK * steps * columns)

    acc, local, heads = call(
        first_kernel,
        shapes(((requests, columns), F32), ((slots, 128), F32), ((256, 256), BF16)),
        cost(STEPS_A),
        adapters,
        table,
        pool,
        tokens,
        weight,
        ins=[HBM] * 5,
        scratch=[*small, pltpu.VMEM(pool.shape, BF16), *parts(STEPS_A)],
        vmem=24,
    )
    acc = pltpu.with_memory_space_constraint(acc, pltpu.HBM)
    part, send = call(
        down_kernel,
        shapes(((slots, 128), F32), ((512, 128), BF16)),
        (1 << 28, 1 << 21),
        received,
        down,
        local,
        heads,
        vmem=8,
    )
    other = lax.ppermute(send, "ctx", [(i, i ^ 1) for i in range(n_ctx)])
    total, pool0, s1, s2, s3 = call(
        middle_kernel,
        shapes(((slots, 128), F32), ((128, 128), BF16), *[((384, 128), BF16)] * 3),
        (1 << 16, 1 << 19),
        part,
        heads,
        other,
        vmem=8,
    )
    r1, r2, r3 = [
        lax.ppermute(s, "ctx", [(i, (i + 2 * j) % n_ctx) for i in range(n_ctx)])
        for j, s in ((1, s1), (2, s2), (3, s3))
    ]
    update = call(
        up_kernel,
        shapes(((slots, columns), BF16))[0],
        (1 << 28, 1 << 21),
        total,
        r1,
        r2,
        r3,
        local,
        up,
        vmem=8,
    )
    returned = lax.all_to_all(
        update.reshape(n_store, CAP, columns), "store", split_axis=0, concat_axis=0, tiled=True
    ).reshape(slots, columns)

    frequency = np.power(
        np.float32(ROPE_THETA), -(np.arange(HEAD // 2, dtype=np.float32) * np.float32(2.0 / HEAD))
    ).astype(np.float32)
    angle = prefix_length.astype(F32)[:, None] * jnp.asarray(frequency)[None, :]
    rest = d_model // BK - STEPS_A
    ids = prefix_block_list.T
    lens = prefix_length.reshape(1, requests)
    aux = call(
        second_kernel,
        shapes(((requests, AUX), F32))[0],
        cost(rest),
        acc,
        dest,
        ids,
        lens,
        jnp.cos(angle),
        jnp.sin(angle),
        tokens,
        weight,
        pool0,
        r1,
        r2,
        r3,
        update,
        ins=[HBM, VMEM, HBM, HBM, VMEM, VMEM, HBM, HBM, VMEM, VMEM, VMEM, VMEM, pl.BlockSpec(memory_space=pl.ANY)],
        scratch=[
            pltpu.VMEM(ids.shape, jnp.int32),
            pltpu.VMEM(lens.shape, jnp.int32),
            pltpu.VMEM((requests, columns), F32),
            *parts(rest),
        ],
        vmem=24,
    )
    out = call(
        attend_kernel,
        shapes(((requests, QUERY_PER_KEY * HEAD), BF16))[0],
        (1 << 28, 1 << 21),
        aux,
        returned,
        vmem=8,
    )
    return out.reshape(requests, 1, QUERY_PER_KEY * HEAD)


def solution(mesh):
    in_specs = (
        P("store", None),
        P(None, "ctx", None),
        P("store", "ctx", None),
        P("store", None, "ctx", None),
        P(),
        P(),
        P("store", None),
        P("store"),
        P(("store", "ctx"), None, None),
    )
    out_specs = P("store", "ctx", None)
    return jax.shard_map(body, mesh=mesh, in_specs=in_specs, out_specs=out_specs, check_vma=False)
```

time: 67 us -> 53.3 us (0.80)
  local copies, waits for them, and re-layouts: 25.4 us -> 0.85 us
  waiting for transfers between devices: 5.79 us -> 16 us
  Pallas kernels: 12.5 us -> 18.2 us
  starting transfers between devices: 20.5 us -> 17.4 us
  other arithmetic: 1.62 us -> 0.31 us
    unnamed x52 -> x12, local copies, waits for them, and re-layouts: 25.4 us -> 0.85 us
    all_to_all x1, waiting for transfers between devices: 0.01 us -> 6.32 us  [body(): lax.all_to_all(update.reshape(n_store, CAP, columns), 'store', split_axis...]
    pallas_call x7, Pallas kernels: 12.5 us -> 18.2 us  [call(): pl.pallas_call(kernel, out_shape=out, name=kernel.__name__, in_specs=ins...]
    all_to_all x1, waiting for transfers between devices: 0.53 us -> 4.45 us  [body(): lax.all_to_all(outgoing.reshape(n_store, CAP, width), 'store', split_axis...]
    all_to_all x1, starting transfers between devices: 6.7 us -> 3.59 us  [body(): lax.all_to_all(update.reshape(n_store, CAP, columns), 'store', split_axis...]
    mul x1 -> x0, other arithmetic: 1.62 us -> none  [body(): jnp.sin(angle)]
  transfers between devices with their start and end apart: 6 -> 6, of which waited for: 4 -> 5; matrix products, arithmetic and copies ran while one was open for 2% -> 1% of each run, Pallas kernels for 11% -> 23%
where the time goes in v2:
time: 53.3 us; the launch traced here: 52.9 us
  Pallas kernels  18.2 us (34%)
  starting transfers between devices  17.4 us (33%)
  waiting for transfers between devices  16 us (30%)
  local copies, waits for them, and re-layouts  0.85 us (2%)
    pallas_call x7, Pallas kernels, call(): pl.pallas_call(kernel, out_shape=out, name=kernel.__name__, in_specs=ins...  18.2 us
    all_to_all x1, starting transfers between devices, body(): lax.all_to_all(outgoing.reshape(n_store, CAP, width), 'store', split_axis...  7.13 us
    ppermute x3, starting transfers between devices, body(): lax.ppermute(s, 'ctx', [(i, (i + 2 * j) % n_ctx) for i in range(n_ctx)])  6.58 us
    all_to_all x1, waiting for transfers between devices, body(): lax.all_to_all(update.reshape(n_store, CAP, columns), 'store', split_axis...  6.32 us
    all_to_all x1, waiting for transfers between devices, body(): lax.all_to_all(outgoing.reshape(n_store, CAP, width), 'store', split_axis...  4.45 us
    ppermute x3, waiting for transfers between devices, body(): lax.ppermute(s, 'ctx', [(i, (i + 2 * j) % n_ctx) for i in range(n_ctx)])  3.92 us
    all_to_all x1, starting transfers between devices, body(): lax.all_to_all(update.reshape(n_store, CAP, columns), 'store', split_axis...  3.59 us
    ppermute x1, waiting for transfers between devices, body(): other = lax.ppermute(send, 'ctx', [(i, i ^ 1) for i in range(n_ctx)])  1.33 us
  transfers between devices with their start and end apart: 6, of which 5 were waited for; matrix products, arithmetic and copies ran while one was open for 1% of the time, Pallas kernels for 23%

profile of v2, /device:TPU:0, one launch (start us, length us, event | category | flops | bytes accessed | tf_op | source)
XLA Modules:
  0.0 52.9 jit_solution(14690999612952041012)
XLA Ops:
  0.0 2.1 %pack_kernel.1 = (bf16[256,1024]{1,0:T(8,128)(2,1)}, s32[8,128]{1,0:T(8,128)S(1)}) custom-call(s32[16,128]{1,0:T(8,128)} %bitcast.24, s32[1,128]{1,0:T(1,128)} %bitcast.26, bf16[128,8192]{1,0:T(8,128)(2,1)} %x_hbm.3), custom_call_target="tpu_custom_call" | custom-call | flops 67108864 | bytes 1048576 | tf_op jit(solution)/shard_map/pack_kernel/pallas_call | solution.py:275
  2.1 7.1 %all-to-all-start = ((bf16[16,16,1024]{2,1,0:T(8,128)(2,1)}), bf16[16,16,1024]{2,1,0:T(8,128)(2,1)S(1)}, u32[]{:S(2)}, u32[]{:S(2)}) async-start(bf16[16,16,1024]{2,1,0:T(8,128)(2,1)} %bitcast.6), calls=%async_computation | async-start | bytes 1048576 | tf_op jit(solution)/shard_map/all_to_all | solution.py:325
  9.3 0.0 copy-start.1
  9.3 6.2 %first_kernel.1 = (f32[128,1280]{1,0:T(8,128)S(1)}, f32[256,128]{1,0:T(8,128)S(1)}, bf16[256,256]{1,0:T(8,128)(2,1)S(1)}) custom-call(s32[16,128]{1,0:T(8,128)} %bitcast.25, s32[1,128]{1,0:T(1,128)} %bitcast.27, bf16[256,256]{1,0:T(8,128)(2,1)} %bitcast.23, bf16[128,8192]{1,0:T(8,128)(2,1)} %x_hbm.3, bf16[8192,1280]{1,0:T(8,128)(2,1)} %bitcast.21), custom_call_target="tpu_custom_call" | custom-call | flops 1342177280 | bytes 10485760 | tf_op jit(solution)/shard_map/first_kernel/pallas_call | solution.py:275
  15.5 0.8 %copy-done.2 = f32[128,1280]{1,0:T(8,128)} copy-done((f32[128,1280]{1,0:T(8,128)}, f32[128,1280]{1,0:T(8,128)S(1)}, u32[]{:S(2)}) %copy-start.2) | copy-done | bytes 655384
  16.3 4.4 %all-to-all-done = bf16[16,16,1024]{2,1,0:T(8,128)(2,1)S(1)} async-done(((bf16[16,16,1024]{2,1,0:T(8,128)(2,1)}), bf16[16,16,1024]{2,1,0:T(8,128)(2,1)S(1)}, u32[]{:S(2)}, u32[]{:S(2)}) %all-to-all-start) | async-done | bytes 524320 | tf_op jit(solution)/shard_map/all_to_all | solution.py:325
  20.7 0.5 %down_kernel.1 = (f32[256,128]{1,0:T(8,128)S(1)}, bf16[512,128]{1,0:T(8,128)(2,1)S(1)}) custom-call(bf16[256,1024]{1,0:T(8,128)(2,1)S(1)} %bitcast.16, bf16[512,1024]{1,0:T(8,128)(2,1)S(1)} %bitcast.18, f32[256,128]{1,0:T(8,128)S(1)} %get-tuple-element.20.local_ref, bf16[256,256]{1,0:T(8,128)(2,1)S(1)} %get-tuple-element.21.heads_ref), custom_call_target="tpu_custom_call" | custom-call | flops 268435456 | bytes 2097152 | tf_op jit(solution)/shard_map/down_kernel/pallas_call | solution.py:275
  21.3 0.1 collective-permute-start
  21.4 1.3 %collective-permute-done.other_ref = bf16[512,128]{1,0:T(8,128)(2,1)S(1)} collective-permute-done((bf16[512,128]{1,0:T(8,128)(2,1)S(1)}, bf16[512,128]{1,0:T(8,128)(2,1)S(1)}, u32[]{:S(2)}, u32[]{:S(2)}) %collective-permute-start) | collective-permute-done | bytes 131104 | tf_op jit(solution)/shard_map/ppermute | solution.py:364
  22.7 0.1 middle_kernel.1
  22.8 2.0 %collective-permute-start.1 = (bf16[384,128]{1,0:T(8,128)(2,1)S(1)}, bf16[384,128]{1,0:T(8,128)(2,1)S(1)}, u32[]{:S(2)}, u32[]{:S(2)}) collective-permute-start(bf16[384,128]{1,0:T(8,128)(2,1)S(1)} %get-tuple-element.25), channel_id=1, source_target_pairs={{0,2},{1,3},{2,4},{3,5},{4,6},{5,7},{6,0},{7,1},{8,10},{9,11},{10,... | collective-permute-start | bytes 294920 | tf_op jit(solution)/shard_map/ppermute | solution.py:375
  24.8 3.6 %collective-permute-start.2 = (bf16[384,128]{1,0:T(8,128)(2,1)S(1)}, bf16[384,128]{1,0:T(8,128)(2,1)S(1)}, u32[]{:S(2)}, u32[]{:S(2)}) collective-permute-start(bf16[384,128]{1,0:T(8,128)(2,1)S(1)} %get-tuple-element.26), channel_id=1, source_target_pairs={{0,4},{1,5},{2,6},{3,7},{4,0},{5,1},{6,2},{7,3},{8,12},{9,13},{10,... | collective-permute-start | bytes 294920 | tf_op jit(solution)/shard_map/ppermute | solution.py:375
  28.4 1.0 %collective-permute-start.3 = (bf16[384,128]{1,0:T(8,128)(2,1)S(1)}, bf16[384,128]{1,0:T(8,128)(2,1)S(1)}, u32[]{:S(2)}, u32[]{:S(2)}) collective-permute-start(bf16[384,128]{1,0:T(8,128)(2,1)S(1)} %get-tuple-element.27), channel_id=1, source_target_pairs={{0,6},{1,7},{2,0},{3,1},{4,2},{5,3},{6,4},{7,5},{8,14},{9,15},{10,... | collective-permute-start | bytes 294920 | tf_op jit(solution)/shard_map/ppermute | solution.py:375
  29.4 0.6 %collective-permute-done.1.r1_ref = bf16[384,128]{1,0:T(8,128)(2,1)S(1)} collective-permute-done((bf16[384,128]{1,0:T(8,128)(2,1)S(1)}, bf16[384,128]{1,0:T(8,128)(2,1)S(1)}, u32[]{:S(2)}, u32[]{:S(2)}) %collective-permute-start.1) | collective-permute-done | bytes 98336 | tf_op jit(solution)/shard_map/ppermute | solution.py:375
  30.0 3.3 %collective-permute-done.2.r2_ref = bf16[384,128]{1,0:T(8,128)(2,1)S(1)} collective-permute-done((bf16[384,128]{1,0:T(8,128)(2,1)S(1)}, bf16[384,128]{1,0:T(8,128)(2,1)S(1)}, u32[]{:S(2)}, u32[]{:S(2)}) %collective-permute-start.2) | collective-permute-done | bytes 98336 | tf_op jit(solution)/shard_map/ppermute | solution.py:375
  33.3 0.0 collective-permute-done.3.r3_ref
  33.3 0.0 copy-done
  33.3 1.4 %up_kernel.1.tie_ref = bf16[256,1280]{1,0:T(8,128)(2,1)} custom-call(f32[256,128]{1,0:T(8,128)S(1)} %get-tuple-element.28.sum_ref, bf16[384,128]{1,0:T(8,128)(2,1)S(1)} %collective-permute-done.1.r1_ref, bf16[384,128]{1,0:T(8,128)(2,1)S(1)} %collective-permute-done.2.r2_ref, bf16[384,128]{1,0:T(8,128)(2,1)S(1)} %collective-permute-done.3.r3_ref, ...), custom_call_target="tpu_custom_call" | custom-call | flops 268435456 | bytes 2097152 | tf_op jit(solution)/shard_map/up_kernel/pallas_call | solution.py:275
  34.8 3.6 %all-to-all-start.1 = ((bf16[16,16,1280]{2,1,0:T(8,128)(2,1)}), bf16[16,16,1280]{2,1,0:T(8,128)(2,1)S(1)}, u32[]{:S(2)}, u32[]{:S(2)}) async-start(bf16[16,16,1280]{2,1,0:T(8,128)(2,1)} %bitcast.11), calls=%async_computation.1 | async-start | bytes 1310720 | tf_op jit(solution)/shard_map/all_to_all | solution.py:390
  38.4 0.0 copy-done.5
  38.4 0.3 multiply_sine_fusion
  38.7 5.9 %second_kernel.1.aux_ref = f32[128,2432]{1,0:T(8,128)S(1)} custom-call(f32[128,1280]{1,0:T(8,128)} %copy-done.2, s32[8,128]{1,0:T(8,128)S(1)} %get-tuple-element.18.dest_ref, s32[8,128]{1,0:T(8,128)S(1)} %bitcast.19, s32[1,128]{1,0:T(1,128)S(1)} %bitcast.20, f32[128,64]{1,0:T(8,128)S(1)} %get-tuple-element.30.cos_ref, ...), custom_call_target="tpu_custom_call" | custom-call | flops 1342177280 | bytes 10485760 | tf_op jit(solution)/shard_map/second_kernel/pallas_call | solution.py:275
  44.7 6.3 %all-to-all-done.1 = bf16[16,16,1280]{2,1,0:T(8,128)(2,1)S(1)} async-done(((bf16[16,16,1280]{2,1,0:T(8,128)(2,1)}), bf16[16,16,1280]{2,1,0:T(8,128)(2,1)S(1)}, u32[]{:S(2)}, u32[]{:S(2)}) %all-to-all-start.1) | async-done | bytes 655392 | tf_op jit(solution)/shard_map/all_to_all | solution.py:390
  51.0 1.9 %attend_kernel.1 = bf16[128,1024]{1,0:T(8,128)(2,1)} custom-call(f32[128,2432]{1,0:T(8,128)S(1)} %second_kernel.1.aux_ref, bf16[256,1280]{1,0:T(8,128)(2,1)S(1)} %bitcast.15), custom_call_target="tpu_custom_call" | custom-call | flops 268435456 | bytes 2097152 | tf_op jit(solution)/shard_map/attend_kernel/pallas_call | solution.py:275
  (9 shorter events, 0.0 us)
Async XLA Ops:
  2.1 18.6 %all-to-all-start = ((bf16[16,16,1024]{2,1,0:T(8,128)(2,1)}), bf16[16,16,1024]{2,1,0:T(8,128)(2,1)S(1)}, u32[]{:S(2)}, u32[]{:S(2)}) async-start(bf16[16,16,1024]{2,1,0:T(8,128)(2,1)} %bitcast.6), calls=%async_computation | async-start | bytes 1048576 | tf_op jit(solution)/shard_map/all_to_all | solution.py:325
  9.3 11.5 %copy-start.1 = (bf16[8,1024,64]{1,2,0:T(8,128)(2,1)S(1)}, bf16[8,1024,64]{1,2,0:T(8,128)(2,1)}, u32[]{:S(2)}) copy-start(bf16[8,1024,64]{1,2,0:T(8,128)(2,1)} %param.12) | copy-start | bytes 3145732
  15.5 0.8 %copy-start.2 = (f32[128,1280]{1,0:T(8,128)}, f32[128,1280]{1,0:T(8,128)S(1)}, u32[]{:S(2)}) copy-start(f32[128,1280]{1,0:T(8,128)S(1)} %get-tuple-element.17.acc_hbm) | copy-start | bytes 1966084
  16.3 17.0 %copy-start = (bf16[8,64,1,1280]{3,1,2,0:T(8,128)(2,1)S(1)}, bf16[8,64,1,1280]{3,1,2,0:T(8,128)(2,1)}, u32[]{:S(2)}) copy-start(bf16[8,64,1,1280]{3,1,2,0:T(8,128)(2,1)} %param.13) | copy-start | bytes 3932164
  21.3 1.4 %collective-permute-start = (bf16[512,128]{1,0:T(8,128)(2,1)S(1)}, bf16[512,128]{1,0:T(8,128)(2,1)S(1)}, u32[]{:S(2)}, u32[]{:S(2)}) collective-permute-start(bf16[512,128]{1,0:T(8,128)(2,1)S(1)} %get-tuple-element.23), channel_id=1, source_target_pairs={{0,1},{1,0},{2,3},{3,2},{4,5},{5,4},{6,7},{7,6},{8,9},{9,8},{10,11... | collective-permute-start | bytes 393224 | tf_op jit(solution)/shard_map/ppermute | solution.py:364
  22.7 15.6 %copy-start.4 = (s32[128]{0:T(128)S(1)}, s32[128]{0:T(128)}, u32[]{:S(2)}) copy-start(s32[128]{0:T(128)} %param.17) | copy-start | bytes 1540
  22.7 15.7 %copy-start.5 = (f32[64]{0:T(128)S(1)}, f32[64]{0:T(128)}, u32[]{:S(2)}) copy-start(f32[64]{0:T(128)} %constant.2.clone) | copy-start | bytes 772
  22.7 16.0 %copy-start.3 = (s32[128,8]{0,1:T(8,128)S(1)}, s32[128,8]{0,1:T(8,128)}, u32[]{:S(2)}) copy-start(s32[128,8]{0,1:T(8,128)} %param.16) | copy-start | bytes 12292
  22.8 7.2 %collective-permute-start.1 = (bf16[384,128]{1,0:T(8,128)(2,1)S(1)}, bf16[384,128]{1,0:T(8,128)(2,1)S(1)}, u32[]{:S(2)}, u32[]{:S(2)}) collective-permute-start(bf16[384,128]{1,0:T(8,128)(2,1)S(1)} %get-tuple-element.25), channel_id=1, source_target_pairs={{0,2},{1,3},{2,4},{3,5},{4,6},{5,7},{6,0},{7,1},{8,10},{9,11},{10,... | collective-permute-start | bytes 294920 | tf_op jit(solution)/shard_map/ppermute | solution.py:375
  24.8 8.5 %collective-permute-start.2 = (bf16[384,128]{1,0:T(8,128)(2,1)S(1)}, bf16[384,128]{1,0:T(8,128)(2,1)S(1)}, u32[]{:S(2)}, u32[]{:S(2)}) collective-permute-start(bf16[384,128]{1,0:T(8,128)(2,1)S(1)} %get-tuple-element.26), channel_id=1, source_target_pairs={{0,4},{1,5},{2,6},{3,7},{4,0},{5,1},{6,2},{7,3},{8,12},{9,13},{10,... | collective-permute-start | bytes 294920 | tf_op jit(solution)/shard_map/ppermute | solution.py:375
  28.4 4.9 %collective-permute-start.3 = (bf16[384,128]{1,0:T(8,128)(2,1)S(1)}, bf16[384,128]{1,0:T(8,128)(2,1)S(1)}, u32[]{:S(2)}, u32[]{:S(2)}) collective-permute-start(bf16[384,128]{1,0:T(8,128)(2,1)S(1)} %get-tuple-element.27), channel_id=1, source_target_pairs={{0,6},{1,7},{2,0},{3,1},{4,2},{5,3},{6,4},{7,5},{8,14},{9,15},{10,... | collective-permute-start | bytes 294920 | tf_op jit(solution)/shard_map/ppermute | solution.py:375
  34.8 16.2 %all-to-all-start.1 = ((bf16[16,16,1280]{2,1,0:T(8,128)(2,1)}), bf16[16,16,1280]{2,1,0:T(8,128)(2,1)S(1)}, u32[]{:S(2)}, u32[]{:S(2)}) async-start(bf16[16,16,1280]{2,1,0:T(8,128)(2,1)} %bitcast.11), calls=%async_computation.1 | async-start | bytes 1310720 | tf_op jit(solution)/shard_map/all_to_all | solution.py:390
